TPU v7x, 256 devices: a whole 4x4x8 slice. The times are simulated.
256 devices in a mesh: seq: 128 (over y, x_lo, z, core), mp: 2 (over x_hi).
Axes of the slice: x: 4 (x_hi: 2, x_lo: 2; x = x_hi * 2 + x_lo), y: 4, z: 8, core: 2. Of those that a mesh axis runs over, the one named last changes fastest.
Arguments:
- normed: bfloat16 [65536, 2048], P('seq', 'mp'), may hold values from -18 to 18
- router: bfloat16 [2048], replicated, may hold values from -0.125 to 0.125
- light_qkv: bfloat16 [3, 2048, 1024], P(None, None, 'mp'), may hold values from -0.125 to 0.125
- light_out: bfloat16 [1024, 2048], P('mp'), may hold values from -0.1875 to 0.1875
- heavy_qkv: bfloat16 [3, 2048, 1024], P(None, 'seq', 'mp'), may hold values from -0.125 to 0.125
- heavy_out: bfloat16 [1024, 2048], P('mp', 'seq'), may hold values from -0.1875 to 0.1875
- query_slots: int32 [128, 32], P('seq'), may hold values from 0 to 511, as said below
- query_count: int32 [128], P('seq'), may hold values from 1 to 32, 2048 in all
- key_slots: int32 [128, 32], P('seq'), may hold values from 0 to 511, as said below
- key_count: int32 [128], P('seq'), may hold values from 1 to 32, 2048 in all
Outputs:
- mixed: bfloat16 [65536, 2048], P('seq', 'mp')
Inputs may be any that keep to these rules, and one draw needn't show every extreme that they name: `query_slots`: each row holds 32 distinct positions of one shard's 512 tokens; only the first query_count entries of a row are live. `key_slots`: each row holds 32 distinct positions of one shard's 512 tokens; only the first key_count entries of a row are live. `query_count`: the counts sum to 2048 and the largest is exactly 32. `key_count`: the counts sum to 2048 and the largest is exactly 32.
All inputs are finite; a program needn't handle non-finite values.
Results may differ from a plain program's by a relative error of at most 0.012.
Values may be sent and summed in bfloat16 or wider, within the bound.
No kernel may reach another device: no remote copies, remote signals or barrier semaphores. Data moves between devices by JAX's collectives and lax.ppermute only.
A program may use at most 128 MiB of HBM per device.

v0:
```python
import jax
import jax.numpy as jnp
from jax import lax
from jax.sharding import PartitionSpec as P

HEAD_DIM = 64
RADIUS = 64


NEG = -1e30


def padded(cells, sides, width):
    for axis, dim in sides:
        count = lax.axis_size(axis)
        ends = count - 1
        head = lax.slice_in_dim(cells, 0, width, axis=dim)
        tail = lax.slice_in_dim(cells, cells.shape[dim] - width, cells.shape[dim], axis=dim)
        cells = jnp.concatenate(
            [
                lax.ppermute(tail, axis, [(i, (i + 1) % count) for i in range(ends)]),
                cells,
                lax.ppermute(head, axis, [((i + 1) % count, i) for i in range(ends)]),
            ],
            axis=dim,
        )
    return cells


def mix_heads(queries, key_rows, value_rows, allowed):
    length = queries.shape[0]
    head_count = queries.shape[1] // HEAD_DIM
    query_heads = queries.reshape(length, head_count, HEAD_DIM)
    key_heads = key_rows.reshape(key_rows.shape[0], head_count, HEAD_DIM)
    value_heads = value_rows.reshape(value_rows.shape[0], head_count, HEAD_DIM)
    scores = jnp.einsum(
        "qhe,khe->hqk", query_heads, key_heads, preferred_element_type=jnp.float32
    ) * HEAD_DIM ** (-0.5)
    scores = jnp.where(allowed[None], scores, NEG)
    row_peak = jnp.max(scores, axis=2, keepdims=True)
    weights = jnp.where(allowed[None], jnp.exp(scores - row_peak), 0.0)
    row_total = jnp.sum(weights, axis=2)
    blended = jnp.einsum(
        "hqk,khe->qhe",
        weights.astype(jnp.bfloat16),
        value_heads,
        preferred_element_type=jnp.float32,
    )
    blended = blended / jnp.transpose(row_total)[:, :, None]
    return blended.reshape(length, head_count * HEAD_DIM).astype(jnp.bfloat16)


def shards(
    normed,
    router,
    light_qkv,
    light_out,
    heavy_qkv,
    heavy_out,
    query_slots,
    query_count,
    key_slots,
    key_count,
):
    local_rows = normed.shape[0]
    shard_index = lax.axis_index("seq")
    shard_total = lax.axis_size("seq")
    capacity = query_slots.shape[1]
    features = lax.all_gather(normed, "mp", axis=1, tiled=True)
    queries = jnp.dot(features, light_qkv[0], preferred_element_type=jnp.float32).astype(
        jnp.bfloat16
    )
    paired = jnp.einsum(
        "td,cdh->cth", features, light_qkv[1:], preferred_element_type=jnp.float32
    ).astype(jnp.bfloat16)
    paired = padded(paired, (("seq", 1),), RADIUS)
    key_rows = paired[0]
    value_rows = paired[1]
    block_rows = min(512, local_rows)
    first_row = shard_index * local_rows
    query_pos = first_row + 0 + jnp.arange(block_rows, dtype=jnp.int32)
    key_pos = first_row + 0 - RADIUS + jnp.arange(block_rows + 2 * RADIUS, dtype=jnp.int32)
    distance = jnp.abs(query_pos[:, None] - key_pos[None, :])
    allowed = (
        (distance <= RADIUS)
        & (key_pos[None, :] >= 0)
        & (key_pos[None, :] < local_rows * shard_total)
    )
    outputs = mix_heads(queries, key_rows, value_rows, allowed)
    light_part = jnp.dot(outputs, light_out, preferred_element_type=jnp.float32)
    slot_range = jnp.arange(capacity, dtype=jnp.int32)
    query_live = slot_range < query_count[0]
    key_live = (slot_range < key_count[0]).astype(jnp.bfloat16)
    query_inputs = features[query_slots[0]]
    key_inputs = features[key_slots[0]]
    portion = lax.all_gather(heavy_qkv, "seq", axis=1, tiled=True)
    heavy_query = jnp.dot(query_inputs, portion[0], preferred_element_type=jnp.float32)
    heavy_key = jnp.dot(key_inputs, portion[1], preferred_element_type=jnp.float32)
    heavy_value = jnp.dot(key_inputs, portion[2], preferred_element_type=jnp.float32)
    heavy_query = heavy_query.astype(jnp.bfloat16)
    heavy_key = heavy_key.astype(jnp.bfloat16)
    heavy_value = heavy_value.astype(jnp.bfloat16)
    head_count = heavy_query.shape[1] // HEAD_DIM
    scale = HEAD_DIM ** (-0.5)
    query_heads = heavy_query.reshape(capacity, head_count, HEAD_DIM)
    row_peak = jnp.full((capacity, head_count), NEG, jnp.float32)
    key_part = lax.all_gather(heavy_key, "seq", axis=0, tiled=True)
    value_part = lax.all_gather(heavy_value, "seq", axis=0, tiled=True)
    live_part = lax.all_gather(key_live, "seq", axis=0, tiled=True)
    length = key_part.shape[0]
    key_heads = key_part.reshape(length, head_count, HEAD_DIM)
    value_heads = value_part.reshape(length, head_count, HEAD_DIM)
    live = live_part[None, None, :] > 0
    scores = (
        jnp.einsum("qhe,khe->qhk", query_heads, key_heads, preferred_element_type=jnp.float32)
        * scale
    )
    scores = jnp.where(live, scores, NEG)
    new_peak = jnp.maximum(row_peak, jnp.max(scores, axis=2))
    weights = jnp.where(live, jnp.exp(scores - new_peak[:, :, None]), 0.0)
    row_total = jnp.sum(weights, axis=2)
    blended = jnp.einsum(
        "qhk,khe->qhe",
        weights.astype(jnp.bfloat16),
        value_heads,
        preferred_element_type=jnp.float32,
    )
    row_peak, row_total, blended = (new_peak, row_total, blended)
    blended = blended / row_total[:, :, None]
    heavy_context = blended.reshape(capacity, head_count * HEAD_DIM).astype(jnp.bfloat16)
    gate = jax.nn.sigmoid(jnp.dot(query_inputs, router, preferred_element_type=jnp.float32))
    gate = jnp.where(query_live, gate, 0.0)
    heavy_rows = (
        jnp.dot(
            heavy_context,
            lax.all_gather(heavy_out, "seq", axis=1, tiled=True),
            preferred_element_type=jnp.float32,
        )
        * gate[:, None]
    )
    combined = light_part.at[query_slots[0]].add(heavy_rows)
    return lax.psum_scatter(combined, "mp", scatter_dimension=1, tiled=True).astype(jnp.bfloat16)


def solution(mesh):
    in_specs = (
        P("seq", "mp"),
        P(),
        P(None, None, "mp"),
        P("mp", None),
        P(None, "seq", "mp"),
        P("mp", "seq"),
        P("seq", None),
        P("seq"),
        P("seq", None),
        P("seq"),
    )
    out_specs = P("seq", "mp")
    return jax.shard_map(shards, mesh=mesh, in_specs=in_specs, out_specs=out_specs, check_vma=False)
```

profile of v0, /device:TPU:1, one launch (start us, length us, event | category | flops | bytes accessed | tf_op | source)
XLA Modules:
  0.0 995.2 jit_solution(5200214284138071772)
XLA Ops:
  6.5 0.0 all-gather.6.cloned.1.call-start
  6.6 0.7 all-gather.6.cloned.1.call-update
  7.3 0.0 all-gather.8.cloned.1.call-start
  7.3 0.7 all-gather.8.cloned.1.call-update
  8.0 0.0 all-gather.12.cloned.1.call-start
  8.1 0.7 fusion.72
  8.7 43.7 %all-gather.6.cloned.1.call-done = bf16[512,2048]{1,0:T(8,128)(2,1)} async-done(((bf16[512,1024]{1,0:T(8,128)(2,1)}), bf16[512,2048]{1,0:T(8,128)(2,1)}) %all-gather.6.cloned.1.call-update) | async-done | bytes 2097168 | tf_op jit(solution)/shard_map/all_gather | solution.py:69
  52.5 2.6 gather_fusion
  55.1 215.8 %all-gather.8.cloned.1.call-done = bf16[3,2048,512]{2,1,0:T(8,128)(2,1)} async-done(((bf16[3,16,512]{2,1,0:T(8,128)(2,1)}), bf16[3,2048,512]{2,1,0:T(8,128)(2,1)}) %all-gather.8.cloned.1.call-update) | async-done | bytes 6291472 | tf_op jit(solution)/shard_map/all_gather | solution.py:96
  270.9 2.7 fusion.56
  273.6 0.0 all-gather.10.cloned.1.call-start
  273.6 2.7 fusion.54
  276.3 0.0 all-gather.14.cloned.1.call-start
  276.4 0.5 all-gather.14.cloned.1.call-update
  276.9 0.0 reduce-scatter.2.cloned.1.call-start
  278.4 0.6 dynamic-slice
  279.6 0.2 dynamic-update-slice
  279.9 280.5 %all-reduce = bf16[4096]{0:T(1024)(128)(2,1)S(1)} all-reduce(bf16[4096]{0:T(1024)(128)(2,1)S(1)} %dynamic-update-slice), channel_id=1, replica_groups=mesh['seq'=128,'mp'=2] {'seq'}, use_global_device_ids=true, to_apply=%add | all-reduce | flops 4096 | bytes 16384
  560.4 1.2 fusion.42
  561.7 5.3 fusion.30
  567.0 0.7 fusion.77
  567.7 1.9 collective-permute-start
  569.6 3.9 collective-permute-start.1
  573.5 3.8 fusion.43
  577.3 2.6 gather_fusion.1
  579.9 0.1 fusion.61
  580.1 0.1 pad_maximum_fusion
  580.2 0.1 fusion.76
  580.3 1.1 copy.17
  581.4 0.3 copy.16
  581.7 8.4 fusion.78
  590.1 4.2 fusion.46
  594.3 3.3 fusion.80
  597.6 2.0 fusion.55
  599.7 0.1 reshape.159
  599.8 6.7 copy.19
  606.5 96.9 %all-gather.10.cloned.1.call-done = bf16[4096,512]{1,0:T(8,128)(2,1)} async-done(((bf16[32,512]{1,0:T(8,128)(2,1)}), bf16[4096,512]{1,0:T(8,128)(2,1)}) %all-gather.10.cloned.1.call-update) | async-done | bytes 4194320 | tf_op jit(solution)/shard_map/all_gather | solution.py:108
  703.4 6.5 copy.18
  709.9 3.2 fusion.79
  713.0 0.9 fusion.11
  713.9 1.3 copy-done.1
  715.2 1.3 fusion.65
  716.6 0.1 convert_element_type.54
  716.7 201.3 %all-gather.14.cloned.1.call-done = bf16[512,2048]{0,1:T(8,128)(2,1)} async-done(((bf16[512,16]{0,1:T(8,128)(2,1)}), bf16[512,2048]{0,1:T(8,128)(2,1)}) %all-gather.14.cloned.1.call-update) | async-done | bytes 2097168 | tf_op jit(solution)/shard_map/all_gather | solution.py:136
  918.0 2.3 convolution_multiply_fusion.1
  920.4 5.1 scatter_fusion
  925.5 60.1 %reduce-scatter.2.cloned.1.call-done = f32[512,1024]{1,0:T(8,128)} async-done(((f32[512,2048]{1,0:T(8,128)}), f32[512,1024]{1,0:T(8,128)}) %reduce-scatter.2.cloned.1.call-update) | async-done | bytes 2097168 | tf_op jit(solution)/shard_map/reduce_scatter | solution.py:142
  985.6 2.7 convert_element_type.55
  (33 shorter events, 0.2 us)
Async XLA Ops:
  6.5 587.8 %copy-start = (bf16[512,2048]{1,0:T(8,128)(2,1)S(1)}, bf16[512,2048]{1,0:T(8,128)(2,1)}, u32[]{:S(2)}) copy-start(bf16[512,2048]{1,0:T(8,128)(2,1)} %param.13) | copy-start | bytes 6291460
  6.5 271.8 %copy-start.7 = (u32[256]{0:T(256)S(1)}, u32[256]{0:T(256)}, u32[]{:S(2)}) copy-start(u32[256]{0:T(256)} %constant.41) | copy-start | bytes 3076
  6.5 271.8 %copy-start.6 = (s32[1,32]{1,0:T(1,128)S(1)}, s32[1,32]{1,0:T(1,128)}, u32[]{:S(2)}) copy-start(s32[1,32]{1,0:T(1,128)} %param.16) | copy-start | bytes 388
  6.5 271.8 %copy-start.3 = (bf16[2048]{0:T(1024)(128)(2,1)S(1)}, bf16[2048]{0:T(1024)(128)(2,1)}, u32[]{:S(2)}) copy-start(bf16[2048]{0:T(1024)(128)(2,1)} %param.11) | copy-start | bytes 12292
  6.5 45.9 %all-gather.6.cloned.1.call-start = ((), (), s32[]{:S(2)}) async-start(), calls=%async_computation.1 | async-start | bytes 3145728 | tf_op jit(solution)/shard_map/all_gather | solution.py:69
  7.3 263.6 %all-gather.8.cloned.1.call-start = ((), (), s32[]{:S(2)}) async-start(), calls=%async_computation.2 | async-start | bytes 6340608 | tf_op jit(solution)/shard_map/all_gather | solution.py:96
  8.0 591.8 %all-gather.12.cloned.1.call-start = ((), (), s32[]{:S(2)}) async-start(), calls=%async_computation.4 | async-start | bytes 4227072 | tf_op jit(solution)/shard_map/all_gather | solution.py:107
  273.6 429.8 %all-gather.10.cloned.1.call-start = ((), (), s32[]{:S(2)}) async-start(), calls=%async_computation.3 | async-start | bytes 4227072 | tf_op jit(solution)/shard_map/all_gather | solution.py:108
  276.3 641.7 %all-gather.14.cloned.1.call-start = ((), (), s32[]{:S(2)}) async-start(), calls=%async_computation.5 | async-start | bytes 2113536 | tf_op jit(solution)/shard_map/all_gather | solution.py:136
  276.9 708.7 %reduce-scatter.2.cloned.1.call-start = ((), (), s32[]{:S(2)}) async-start(), calls=%async_computation.6 | async-start | bytes 6291456 | tf_op jit(solution)/shard_map/reduce_scatter | solution.py:142
  278.3 282.1 %copy-start.4 = (s32[32]{0:T(128)}, s32[32]{0:T(128)S(1)}, u32[]{:S(2)}) copy-start(s32[32]{0:T(128)S(1)} %fusion.71) | copy-start | bytes 388
  561.7 11.9 %copy-start.2 = (bf16[512,2048]{1,0:T(8,128)(2,1)S(1)}, bf16[512,2048]{1,0:T(8,128)(2,1)}, u32[]{:S(2)}) copy-start(bf16[512,2048]{1,0:T(8,128)(2,1)} %all-gather.6.cloned.1.call-done) | copy-start | bytes 6291460
  567.7 12.4 %collective-permute-start = (bf16[2,64,512]{2,1,0:T(8,128)(2,1)}, bf16[2,64,512]{2,1,0:T(8,128)(2,1)S(1)}, u32[]{:S(2)}, u32[]{:S(2)}) collective-permute-start(bf16[2,64,512]{2,1,0:T(8,128)(2,1)} %get-tuple-element.7), channel_id=1, source_target_pairs={{0,2},{2,4},{4,6},{6,8},{8,10},{10,12},{12,14},{14,16},{16,18},{18... | collective-permute-start | bytes 393224 | tf_op jit(solution)/shard_map/ppermute | solution.py:21
  569.6 10.5 %collective-permute-start.1 = (bf16[2,64,512]{2,1,0:T(8,128)(2,1)}, bf16[2,64,512]{2,1,0:T(8,128)(2,1)S(1)}, u32[]{:S(2)}, u32[]{:S(2)}) collective-permute-start(bf16[2,64,512]{2,1,0:T(8,128)(2,1)} %get-tuple-element.8), channel_id=1, source_target_pairs={{2,0},{4,2},{6,4},{8,6},{10,8},{12,10},{14,12},{16,14},{18,16},{20... | collective-permute-start | bytes 393224 | tf_op jit(solution)/shard_map/ppermute | solution.py:23
  713.0 2.2 copy-start.1
  715.2 205.1 %copy-start.5 = (s32[32]{0:T(128)S(1)}, s32[32]{0:T(128)}, u32[]{:S(2)}) copy-start(s32[32]{0:T(128)} %copy-done.4) | copy-start | bytes 388
Sparse Core Ops, SparseCore 0:
  9.1 43.2 all-gather.5
  54.4 216.4 all-gather.7
  273.7 213.8 all-gather.11
  489.3 214.0 all-gather.9
  705.1 212.8 all-gather.13
  925.6 59.9 reduce-scatter.1
where the time goes:
time: 996 us; the launch traced here: 995 us
  waiting for transfers between devices  620 us (62%)
  blocking collectives  281 us (28%)
  matrix products  39.3 us (4%)
  local copies, waits for them, and re-layouts  23 us (2%)
  between operations  15.7 us (2%)
  other arithmetic  10.8 us (1%)
    unnamed x1, blocking collectives  281 us
    all_gather x1, waiting for transfers between devices, shards(): portion = lax.all_gather(heavy_qkv, 'seq', axis=1, tiled=True)  216 us
    all_gather x1, waiting for transfers between devices, shards(): lax.all_gather(heavy_out, 'seq', axis=1, tiled=True)  201 us
    all_gather x1, waiting for transfers between devices, shards(): value_part = lax.all_gather(heavy_value, 'seq', axis=0, tiled=True)  96.9 us
    reduce_scatter x1, waiting for transfers between devices, shards(): lax.psum_scatter(combined, 'mp', scatter_dimension=1, tiled=True)  60.1 us
    all_gather x1, waiting for transfers between devices, shards(): features = lax.all_gather(normed, 'mp', axis=1, tiled=True)  43.7 us
  transfers between devices with their start and end apart: 8, of which 5 were waited for; matrix products, arithmetic and copies ran while one was open for 6% of the time, Pallas kernels for 0%

commit v1 on v0

v1 whole, which is shorter than its diff:
```python
import functools

import jax
import jax.numpy as jnp
from jax import lax
from jax.experimental import pallas as pl
from jax.experimental.pallas import tpu as pltpu
from jax.sharding import Mesh
from jax.sharding import PartitionSpec as P

HEAD_DIM = 64
RADIUS = 64
NEG = -1e30
SEQ = ("y", "xl", "z", "c")
GROUP = ("y", "xl")


NT = (((1,), (1,)), ((), ()))


def spec(shape, index):
    return pl.BlockSpec(shape, index)


def project_own_kernel(pos, x_ref, w_ref, out_ref):
    out_ref[0] = jnp.dot(x_ref[...], w_ref[0], preferred_element_type=jnp.float32)


def project_own(pos, x, w):
    rows, half = x.shape
    cols = w.shape[2]
    return pl.pallas_call(
        project_own_kernel,
        out_shape=jax.ShapeDtypeStruct((3, rows, cols), jnp.float32),
        grid_spec=pltpu.PrefetchScalarGridSpec(
            num_scalar_prefetch=1,
            grid=(3,),
            in_specs=[
                spec((rows, half), lambda j, p: (0, 0)),
                spec((1, half, cols), lambda j, p: (j, p[1], 0)),
            ],
            out_specs=spec((1, rows, cols), lambda j, p: (j, 0, 0)),
        ),
        name="light_project_own",
    )(pos, x, w)


def project_add_kernel(pos, x_ref, w_ref, part_ref, out_ref):
    total = jnp.dot(x_ref[...], w_ref[0], preferred_element_type=jnp.float32) + part_ref[0]
    out_ref[0] = total.astype(jnp.bfloat16)


def project_add(pos, x, w, part, first, count):
    rows, half = x.shape
    cols = w.shape[2]
    return pl.pallas_call(
        project_add_kernel,
        out_shape=jax.ShapeDtypeStruct((count, rows, cols), jnp.bfloat16),
        grid_spec=pltpu.PrefetchScalarGridSpec(
            num_scalar_prefetch=1,
            grid=(count,),
            in_specs=[
                spec((rows, half), lambda j, p: (0, 0)),
                spec((1, half, cols), lambda j, p: (j + first, 1 - p[1], 0)),
                spec((1, rows, cols), lambda j, p: (j + first, 0, 0)),
            ],
            out_specs=spec((1, rows, cols), lambda j, p: (j, 0, 0)),
        ),
        name="light_project_add",
    )(pos, x, w, part)


def light_kernel(pos, q_ref, kv_ref, left_ref, right_ref, own_w_ref, other_w_ref, own_ref, other_ref, pad_ref, *, tokens):
    step = pl.program_id(0)
    block = q_ref.shape[1]
    length = kv_ref.shape[1]
    width = q_ref.shape[2]
    span = block + 2 * RADIUS

    @pl.when(step == 0)
    def _():
        pad_ref[:, 0:RADIUS, :] = left_ref[...]
        pad_ref[:, RADIUS : RADIUS + length, :] = kv_ref[...]
        pad_ref[:, RADIUS + length :, :] = right_ref[...]

    start = pl.multiple_of(step * block, block)
    row = lax.broadcasted_iota(jnp.int32, (block, span), 0)
    col = lax.broadcasted_iota(jnp.int32, (block, span), 1)
    key = pos[0] * length + step * block - RADIUS + col
    allowed = (col >= row) & (col - row <= 2 * RADIUS) & (key >= 0) & (key < tokens)
    bias = jnp.where(allowed, 0.0, NEG)
    bias = jnp.concatenate([bias, bias], axis=0)
    lane = lax.broadcasted_iota(jnp.int32, (block, 2 * HEAD_DIM), 1)
    first = lane < HEAD_DIM
    pieces = []
    for pair in range(width // (2 * HEAD_DIM)):
        lanes = slice(pair * 2 * HEAD_DIM, (pair + 1) * 2 * HEAD_DIM)
        q = q_ref[0, :, lanes]
        k = pad_ref[0, pl.ds(start, span), lanes]
        v = pad_ref[1, pl.ds(start, span), lanes]
        zero = jnp.zeros_like(q)
        both = jnp.concatenate([jnp.where(first, q, zero), jnp.where(first, zero, q)], axis=0)
        scores = lax.dot_general(both, k, NT, preferred_element_type=jnp.float32)
        scores = scores * (HEAD_DIM ** -0.5) + bias
        peak = jnp.max(scores, axis=1, keepdims=True)
        weights = jnp.exp(scores - peak)
        total = jnp.sum(weights, axis=1, keepdims=True)
        blended = jnp.dot(weights.astype(jnp.bfloat16), v, preferred_element_type=jnp.float32) / total
        pieces.append(jnp.where(first, blended[:block], blended[block:]).astype(jnp.bfloat16))
    context = jnp.concatenate(pieces, axis=1)
    other_ref[...] = jnp.dot(context, other_w_ref[...], preferred_element_type=jnp.float32).astype(jnp.bfloat16)
    own_ref[...] = jnp.dot(context, own_w_ref[...], preferred_element_type=jnp.float32)


def light_attention(pos, q, kv, left, right, w, tokens):
    rows, width = q.shape[1:]
    half = w.shape[1] // 2
    block = 128
    return pl.pallas_call(
        functools.partial(light_kernel, tokens=tokens),
        out_shape=(
            jax.ShapeDtypeStruct((rows, half), jnp.float32),
            jax.ShapeDtypeStruct((rows, half), jnp.bfloat16),
        ),
        grid_spec=pltpu.PrefetchScalarGridSpec(
            num_scalar_prefetch=1,
            grid=(rows // block,),
            in_specs=[
                spec((1, block, width), lambda b, p: (0, b, 0)),
                spec((2, rows, width), lambda b, p: (0, 0, 0)),
                spec((2, RADIUS, width), lambda b, p: (0, 0, 0)),
                spec((2, RADIUS, width), lambda b, p: (0, 0, 0)),
                spec((width, half), lambda b, p: (0, p[1])),
                spec((width, half), lambda b, p: (0, 1 - p[1])),
            ],
            out_specs=(
                spec((block, half), lambda b, p: (b, 0)),
                spec((block, half), lambda b, p: (b, 0)),
            ),
            scratch_shapes=[pltpu.VMEM((2, rows + 2 * RADIUS, width), jnp.bfloat16)],
        ),
        name="light_attention",
    )(pos, q, kv, left, right, w, w)


def pack_heads_kernel(count, qkv_ref, out_w_ref, packed_ref):
    depth = qkv_ref.shape[1]
    heads = qkv_ref.shape[2] // HEAD_DIM
    row = lax.broadcasted_iota(jnp.int32, (depth, depth), 0)
    col = lax.broadcasted_iota(jnp.int32, (depth, depth), 1)
    eye = jnp.where(row == col, 1.0, 0.0).astype(jnp.bfloat16)
    turned = lax.dot_general(eye, out_w_ref[...], NT, preferred_element_type=jnp.float32).astype(jnp.bfloat16)
    marks = jnp.full((packed_ref.shape[1] - depth, packed_ref.shape[2]), count[0], jnp.int32)
    marks = marks.astype(jnp.float32).astype(jnp.bfloat16)
    for h in range(heads):
        lanes = slice(h * HEAD_DIM, (h + 1) * HEAD_DIM)
        piece = jnp.concatenate([qkv_ref[0, :, lanes], turned[:, lanes], qkv_ref[1, :, lanes], qkv_ref[2, :, lanes]], axis=1)
        for side in range(2):
            packed_ref[2 * h + side, 0:depth, :] = piece
            packed_ref[2 * h + side, depth:, :] = marks


def pack_heads(count, qkv, out_w):
    depth = qkv.shape[1]
    heads = qkv.shape[2] // HEAD_DIM
    return pl.pallas_call(
        pack_heads_kernel,
        out_shape=jax.ShapeDtypeStruct((2 * heads, depth + 8, 4 * HEAD_DIM), jnp.bfloat16),
        grid_spec=pltpu.PrefetchScalarGridSpec(
            num_scalar_prefetch=1,
            grid=(1,),
            in_specs=[spec(qkv.shape, lambda i, p: (0, 0, 0)), spec(out_w.shape, lambda i, p: (0, 0))],
            out_specs=spec((2 * heads, depth + 8, 4 * HEAD_DIM), lambda i, p: (0, 0, 0)),
        ),
        name="pack_heads",
    )(count, qkv, out_w)


def pack_copies_kernel(pos, in_ref, out_ref, *, depth):
    side = pos[1]
    copies = out_ref.shape[0]
    group = in_ref.shape[0] // 2
    lane = lax.broadcasted_iota(jnp.int32, (depth, 4 * HEAD_DIM), 1)
    from_out = (lane >= HEAD_DIM) & (lane < 2 * HEAD_DIM)
    marks = []
    for i in range(group):
        qkv = in_ref[side * group + i, 0:depth, :]
        out_w = in_ref[2 * i + side, 0:depth, :]
        tile = jnp.where(from_out, out_w, qkv)
        marks.append(in_ref[2 * i + side, depth : depth + 1, :])
        for t in range(copies):
            out_ref[t, i * depth : (i + 1) * depth, :] = tile
    marks = jnp.concatenate(marks, axis=0)
    for t in range(copies):
        out_ref[t, group * depth :, :] = marks


def pack_copies(pos, sliced, copies):
    group = sliced.shape[0] // 2
    depth = sliced.shape[1] - 8
    shape = (copies, group * depth + group, 4 * HEAD_DIM)
    return pl.pallas_call(
        functools.partial(pack_copies_kernel, depth=depth),
        out_shape=jax.ShapeDtypeStruct(shape, jnp.bfloat16),
        grid_spec=pltpu.PrefetchScalarGridSpec(
            num_scalar_prefetch=1,
            grid=(1,),
            in_specs=[spec(sliced.shape, lambda i, p: (0, 0, 0))],
            out_specs=spec(shape, lambda i, p: (0, 0, 0)),
        ),
        name="pack_copies",
    )(pos, sliced)


def heavy_project_kernel(pos, mine_ref, theirs_ref, r0, r1, r2, r3, own_ref, other_ref, w_ref, *, depth, capacity):
    side, core, y, xl = pos[1], pos[2], pos[3], pos[4]
    z_size = mine_ref.shape[0]
    for y_half in range(2):
        for x in range(2):
            for m in range(2):
                i = (y_half * 2 + x) * 2 + m
                for z in range(z_size):
                    base = ((y_half * 2 + x) * z_size + z) * 2
                    w_ref[m, pl.ds(pl.multiple_of((base + core) * depth, depth), depth), :] = mine_ref[
                        z, i * depth : (i + 1) * depth, :
                    ]
                    w_ref[m, pl.ds(pl.multiple_of((base + 1 - core) * depth, depth), depth), :] = theirs_ref[
                        z, i * depth : (i + 1) * depth, :
                    ]
    lane = lax.broadcasted_iota(jnp.int32, (capacity, 2 * HEAD_DIM), 1)
    keep = lane < HEAD_DIM
    for target, w in ((other_ref, w_ref[1 - side]), (own_ref, w_ref[side])):
        for d, piece in enumerate((r0, r1, r2, r3)):
            rows = piece[...].reshape(4 * capacity, piece.shape[2])
            result = jnp.dot(rows, w, preferred_element_type=jnp.float32)
            source_y = lax.rem(y - d + 4, 4)
            for which in range(2):
                source = source_y * 2 + (xl if which == 0 else 1 - xl)
                top = which * 2 * capacity
                query = jnp.where(keep, result[top : top + capacity, : 2 * HEAD_DIM], 0.0)
                keys = result[top + capacity : top + 2 * capacity, 2 * HEAD_DIM :]
                value = jnp.concatenate([query, keys], axis=1)
                target[pl.ds(pl.multiple_of(source * capacity, capacity), capacity), :] = value.astype(target.dtype)


def heavy_project(pos, mine, theirs, pieces, depth):
    capacity = pieces[0].shape[1] // 2
    half = pieces[0].shape[2]
    slots = 8 * capacity
    whole3 = lambda i, p: (0, 0, 0)
    return pl.pallas_call(
        functools.partial(heavy_project_kernel, depth=depth, capacity=capacity),
        out_shape=(
            jax.ShapeDtypeStruct((slots, 4 * HEAD_DIM), jnp.float32),
            jax.ShapeDtypeStruct((slots, 4 * HEAD_DIM), jnp.bfloat16),
        ),
        grid_spec=pltpu.PrefetchScalarGridSpec(
            num_scalar_prefetch=1,
            grid=(1,),
            in_specs=[spec(mine.shape, whole3), spec(theirs.shape, whole3)] + [spec(p.shape, whole3) for p in pieces],
            out_specs=(
                spec((slots, 4 * HEAD_DIM), lambda i, p: (0, 0)),
                spec((slots, 4 * HEAD_DIM), lambda i, p: (0, 0)),
            ),
            scratch_shapes=[pltpu.VMEM((2, half, 4 * HEAD_DIM), jnp.bfloat16)],
        ),
        name="heavy_project",
    )(pos, mine, theirs, *pieces)


def finish_kernel(own_ref, arrived_ref, query_ref, copies_ref):
    total = (own_ref[...] + arrived_ref[...].astype(jnp.float32)).astype(jnp.bfloat16)
    query_ref[...] = total[:, : 2 * HEAD_DIM]
    for t in range(copies_ref.shape[0]):
        copies_ref[t] = total[:, 2 * HEAD_DIM :]


def finish(own, arrived, copies):
    slots = own.shape[0]
    return pl.pallas_call(
        finish_kernel,
        out_shape=(
            jax.ShapeDtypeStruct((slots, 2 * HEAD_DIM), jnp.bfloat16),
            jax.ShapeDtypeStruct((copies, slots, 2 * HEAD_DIM), jnp.bfloat16),
        ),
        name="heavy_finish",
    )(own, arrived)


def out_weights_kernel(pos, mine_ref, theirs_ref, out_ref, *, depth):
    core = pos[2]
    z_size = mine_ref.shape[0]
    for i in range(8):
        for z in range(z_size):
            base = (i * z_size + z) * 2
            out_ref[pl.ds(pl.multiple_of((base + core) * depth, depth), depth), :] = mine_ref[
                z, i * depth : (i + 1) * depth, :
            ]
            out_ref[pl.ds(pl.multiple_of((base + 1 - core) * depth, depth), depth), :] = theirs_ref[
                z, i * depth : (i + 1) * depth, :
            ]


def out_weights(pos, mine, theirs, depth):
    z_size = mine.shape[0]
    shape = (16 * z_size * depth, 2 * HEAD_DIM)
    block = (z_size, mine.shape[1], 2 * HEAD_DIM)
    return pl.pallas_call(
        functools.partial(out_weights_kernel, depth=depth),
        out_shape=jax.ShapeDtypeStruct(shape, jnp.bfloat16),
        grid_spec=pltpu.PrefetchScalarGridSpec(
            num_scalar_prefetch=1,
            grid=(1,),
            in_specs=[spec(block, lambda i, p: (0, 0, 0))] * 2,
            out_specs=spec(shape, lambda i, p: (0, 0)),
        ),
        name="out_weights",
    )(pos, mine, theirs)


def heavy_kernel(q_ref, own_ref, other_ref, bias_ref, w_ref, out_ref):
    keys = own_ref.shape[0]
    q = q_ref[...]
    lane = lax.broadcasted_iota(jnp.int32, (1, 2 * HEAD_DIM), 1)
    scale = HEAD_DIM ** -0.5
    s0 = lax.dot_general(q, own_ref[...], NT, preferred_element_type=jnp.float32) * scale + bias_ref[:, :keys]
    s1 = lax.dot_general(q, other_ref[...], NT, preferred_element_type=jnp.float32) * scale + bias_ref[:, keys:]
    peak = jnp.maximum(jnp.max(s0, axis=1, keepdims=True), jnp.max(s1, axis=1, keepdims=True))
    p0 = jnp.exp(s0 - peak)
    p1 = jnp.exp(s1 - peak)
    total = jnp.sum(p0, axis=1, keepdims=True) + jnp.sum(p1, axis=1, keepdims=True)
    blended = jnp.dot(p0.astype(jnp.bfloat16), own_ref[...], preferred_element_type=jnp.float32)
    blended = blended + jnp.dot(p1.astype(jnp.bfloat16), other_ref[...], preferred_element_type=jnp.float32)
    context = jnp.where(lane >= HEAD_DIM, blended / total, 0.0).astype(jnp.bfloat16)
    part = lax.dot_general(context, w_ref[...], NT, preferred_element_type=jnp.float32).astype(jnp.bfloat16)
    count, capacity, half = out_ref.shape
    for i in range(count):
        top = i // 2 * capacity
        out_ref[i] = part[top : top + capacity, i % 2 * half : (i % 2 + 1) * half]


def heavy_attention(q, own, other, bias, w, group):
    return pl.pallas_call(
        heavy_kernel,
        out_shape=jax.ShapeDtypeStruct((2 * group, q.shape[0] // group, w.shape[0] // 2), jnp.bfloat16),
        name="heavy_attention",
    )(q, own, other, bias, w)


def combine_kernel(own_ref, recv_ref, parts_ref, logit_ref, live_ref, slots_ref, out_ref, hi_ref, lo_ref):
    step = pl.program_id(0)
    block = own_ref.shape[0]

    @pl.when(step == 0)
    def _():
        total = parts_ref[0].astype(jnp.float32)
        for i in range(1, parts_ref.shape[0]):
            total = total + parts_ref[i].astype(jnp.float32)
        gate = jnp.where(live_ref[...] > 0, 1.0 / (1.0 + jnp.exp(-logit_ref[...])), 0.0)
        total = total * gate[:, 0:1]
        hi = total.astype(jnp.bfloat16)
        hi_ref[...] = hi
        lo_ref[...] = (total - hi.astype(jnp.float32)).astype(jnp.bfloat16)

    capacity = slots_ref.shape[1]
    token = lax.broadcasted_iota(jnp.int32, (block, capacity), 0) + step * block
    pick = jnp.where(token == slots_ref[...], 1.0, 0.0).astype(jnp.bfloat16)
    heavy = jnp.dot(pick, hi_ref[...], preferred_element_type=jnp.float32)
    heavy = heavy + jnp.dot(pick, lo_ref[...], preferred_element_type=jnp.float32)
    out_ref[...] = (own_ref[...] + recv_ref[...].astype(jnp.float32) + heavy).astype(jnp.bfloat16)


def combine(own, recv, parts, logit, live, slots):
    rows, cols = own.shape
    capacity = slots.shape[1]
    block = 128
    return pl.pallas_call(
        combine_kernel,
        out_shape=jax.ShapeDtypeStruct((rows, cols), jnp.bfloat16),
        grid=(rows // block,),
        in_specs=[
            spec((block, cols), lambda b: (b, 0)),
            spec((block, cols), lambda b: (b, 0)),
            spec(parts.shape, lambda b: (0, 0, 0)),
            spec((capacity, 128), lambda b: (0, 0)),
            spec((capacity, 128), lambda b: (0, 0)),
            spec((1, capacity), lambda b: (0, 0)),
        ],
        out_specs=spec((block, cols), lambda b: (b, 0)),
        scratch_shapes=[
            pltpu.VMEM((capacity, cols), jnp.bfloat16),
            pltpu.VMEM((capacity, cols), jnp.bfloat16),
        ],
        name="combine",
    )(own, recv, parts, logit, live, slots)


def swap(a, axis):
    return lax.ppermute(a, axis, [(0, 1), (1, 0)])


def layer(
    normed,
    router,
    light_qkv,
    light_out,
    heavy_qkv,
    heavy_out,
    query_slots,
    query_count,
    key_slots,
    key_count,
):
    rows, half = normed.shape
    side = lax.axis_index("xh")
    core = lax.axis_index("c")
    shard_index = lax.axis_index(SEQ)
    shard_total = lax.axis_size(SEQ)
    y_size, _, z_size, _ = (lax.axis_size(axis) for axis in SEQ)
    capacity = query_slots.shape[1]
    feature_rows = heavy_qkv.shape[1]
    heads = heavy_qkv.shape[2] // HEAD_DIM
    group = heads
    pos = jnp.stack([shard_index, side, core, lax.axis_index("y"), lax.axis_index("xl")]).astype(jnp.int32)

    slots = jnp.concatenate([query_slots[0], key_slots[0]])
    pick = (slots[:, None] == jnp.arange(rows, dtype=jnp.int32)[None, :]).astype(jnp.bfloat16)
    routed = jnp.dot(pick, normed, preferred_element_type=jnp.float32).astype(jnp.bfloat16)
    partner = swap(routed, "xl")
    pair = jnp.stack([routed, partner])
    pieces = [pair]
    for d in range(1, y_size):
        pieces.append(lax.ppermute(pair, "y", [(i, (i + d) % y_size) for i in range(y_size)]))

    by_head = pack_heads(key_count, heavy_qkv, heavy_out)
    sliced = lax.all_to_all(by_head, GROUP + ("xh",), 0, 0)
    packed = pack_copies(pos, sliced, z_size)
    mine = lax.all_to_all(packed, "z", 0, 0)
    theirs = swap(mine, "c")
    out_all = out_weights(pos, mine, theirs, feature_rows)

    tail = group * feature_rows
    all_counts = jnp.stack([mine[:, tail:, 0], theirs[:, tail:, 0]], axis=0)
    slot_range = jnp.arange(capacity, dtype=jnp.int32)
    live = slot_range[None, None, None, :] < all_counts.astype(jnp.int32)[..., None]
    bias = jnp.where(live, 0.0, NEG).astype(jnp.float32).reshape(1, shard_total * capacity)

    part_own, part_other = heavy_project(pos, mine, theirs, pieces, feature_rows)
    arrived = swap(part_other, "xh")
    query, copies = finish(part_own, arrived, z_size)
    keys_own = lax.all_to_all(copies, "z", 0, 0)
    keys_other = swap(keys_own, "c")
    keys_own = keys_own.reshape(-1, 2 * HEAD_DIM)
    keys_other = keys_other.reshape(-1, 2 * HEAD_DIM)
    outputs = heavy_attention(query, keys_own, keys_other, bias, out_all, group)
    parts = lax.all_to_all(outputs, GROUP + ("xh",), 0, 0)

    features = swap(normed, "xh")
    partial = project_own(pos, normed, light_qkv)
    paired = project_add(pos, features, light_qkv, partial, 1, 2)
    ends = shard_total - 1
    left = lax.ppermute(paired[:, rows - RADIUS :], SEQ, [(i, i + 1) for i in range(ends)])
    right = lax.ppermute(paired[:, :RADIUS], SEQ, [(i + 1, i) for i in range(ends)])
    queries = project_add(pos, features, light_qkv, partial, 0, 1)
    own, other = light_attention(pos, queries, paired, left, right, light_out, rows * shard_total)
    recv = swap(other, "xh")

    picked = jnp.dot(pick[:capacity], features, preferred_element_type=jnp.float32)
    router_own = lax.dynamic_slice_in_dim(router, side * half, half, 0).astype(jnp.float32)
    router_other = lax.dynamic_slice_in_dim(router, (1 - side) * half, half, 0).astype(jnp.float32)
    logit = jnp.sum(routed[:capacity].astype(jnp.float32) * router_own[None], axis=1)
    logit = logit + jnp.sum(picked * router_other[None], axis=1)
    logit = jnp.broadcast_to(logit[:, None], (capacity, 128))
    query_live = jnp.broadcast_to((slot_range < query_count[0]).astype(jnp.float32)[:, None], (capacity, 128))
    return combine(own, recv, parts, logit, query_live, query_slots)


def solution(mesh):
    fine = Mesh(mesh.devices.reshape(4, 2, 8, 2, 2), SEQ + ("xh",))
    in_specs = (
        P(SEQ, "xh"),
        P(),
        P(None, None, "xh"),
        P("xh", None),
        P(None, SEQ, "xh"),
        P("xh", SEQ),
        P(SEQ, None),
        P(SEQ),
        P(SEQ, None),
        P(SEQ),
    )
    return jax.shard_map(layer, mesh=fine, in_specs=in_specs, out_specs=P(SEQ, "xh"), check_vma=False)
```

time: 996 us -> 172 us (0.17)
  waiting for transfers between devices: 620 us -> 66.3 us
  blocking collectives: 281 us -> 0 us
  Pallas kernels: 0 us -> 45.9 us
  matrix products: 39.3 us -> 1.94 us
  starting transfers between devices: 6.05 us -> 41.8 us
  between operations: 15.7 us -> 1.61 us
  local copies, waits for them, and re-layouts: 23 us -> 12.8 us
    all_gather x5 -> x0, waiting for transfers between devices: 558 us -> none  [the longest x1 216 us: shards(): portion = lax.all_gather(heavy_qkv, 'seq', axis=1, tiled=True)]
    unnamed x1 -> x0, blocking collectives: 281 us -> none
    reduce_scatter x1 -> x0, waiting for transfers between devices: 60.1 us -> none  [shards(): lax.psum_scatter(combined, 'mp', scatter_dimension=1, tiled=True)]
    pallas_call x0 -> x11, Pallas kernels: none -> 45.9 us  [the longest x2 8.84 us: project_add(): pl.pallas_call(project_add_kernel, out_shape=jax.ShapeDtypeStruct((count,...]
    all_to_all x0 -> x4, waiting for transfers between devices: none -> 34.2 us  [the longest x1 15.6 us: layer(): mine = lax.all_to_all(packed, 'z', 0, 0)]
    ppermute x2 -> x11, waiting for transfers between devices: 0.01 us -> 32 us  [the longest x6 19.1 us: swap(): return lax.ppermute(a, axis, [(0, 1), (1, 0)])]
    dot_general x11 -> x2, matrix products: 30.9 us -> 1.94 us  [the longest x1 1.56 us: layer(): jnp.dot(pick, normed, preferred_element_type=jnp.float32)]
    all_to_all x0 -> x4, starting transfers between devices: none -> 25.1 us  [the longest x1 8.19 us: layer(): mine = lax.all_to_all(packed, 'z', 0, 0)]
  transfers between devices with their start and end apart: 8 -> 15, of which waited for: 5 -> 9; matrix products, arithmetic and copies ran while one was open for 6% -> 4% of each run, Pallas kernels for 0% -> 21%
where the time goes in v1:
time: 172 us; the launch traced here: 171 us
  waiting for transfers between devices  66.3 us (39%)
  Pallas kernels  45.9 us (27%)
  starting transfers between devices  41.8 us (24%)
  local copies, waits for them, and re-layouts  12.8 us (7%)
  matrix products  1.94 us (1%)
    ppermute x6, waiting for transfers between devices, swap(): return lax.ppermute(a, axis, [(0, 1), (1, 0)])  19.1 us
    all_to_all x1, waiting for transfers between devices, layer(): mine = lax.all_to_all(packed, 'z', 0, 0)  15.6 us
    ppermute x3, waiting for transfers between devices, layer(): lax.ppermute(pair, 'y', [(i, (i + d) % y_size) for i in range(y_size)])  12.9 us
    all_to_all x1, waiting for transfers between devices, layer(): parts = lax.all_to_all(outputs, GROUP + ('xh',), 0, 0)  12.1 us
    pallas_call x2, Pallas kernels, project_add(): pl.pallas_call(project_add_kernel, out_shape=jax.ShapeDtypeStruct((count,...  8.84 us
    pallas_call x1, Pallas kernels, light_attention(): pl.pallas_call(functools.partial(light_kernel, tokens=tokens), out_shape=...  8.52 us
    all_to_all x1, starting transfers between devices, layer(): mine = lax.all_to_all(packed, 'z', 0, 0)  8.19 us
    all_to_all x1, starting transfers between devices, layer(): sliced = lax.all_to_all(by_head, GROUP + ('xh',), 0, 0)  7.57 us
  transfers between devices with their start and end apart: 15, of which 9 were waited for; matrix products, arithmetic and copies ran while one was open for 4% of the time, Pallas kernels for 21%

profile of v1, /device:TPU:1, one launch (start us, length us, event | category | flops | bytes accessed | tf_op | source)
XLA Modules:
  0.0 171.4 jit_solution(2330513000253252244)
XLA Ops:
  0.7 1.5 copy.12.out_w_ref
  2.2 1.8 %pack_heads.1 = bf16[16,24,256]{2,1,0:T(8,128)(2,1)} custom-call(s32[1]{0:T(128)S(6)} %copy.15.count, bf16[3,16,512]{2,1,0:T(8,128)(2,1)} %qkv_ref.1, bf16[512,16]{1,0:T(8,128)(2,1)} %copy.12.out_w_ref), custom_call_target="tpu_custom_call" | custom-call | tf_op jit(solution)/shard_map/pack_heads/pallas_call | solution.py:166
  4.1 7.6 %all-to-all-start = ((bf16[16,24,256]{2,1,0:T(8,128)(2,1)}), bf16[16,24,256]{2,1,0:T(8,128)(2,1)S(1)}, u32[]{:S(2)}, u32[]{:S(2)}) async-start(bf16[16,24,256]{2,1,0:T(8,128)(2,1)} %pack_heads.1), calls=%async_computation | async-start | bytes 393216 | tf_op jit(solution)/shard_map/all_to_all | solution.py:436
  12.3 6.6 %all-to-all-done.in_ref = bf16[16,24,256]{2,1,0:T(8,128)(2,1)S(1)} async-done(((bf16[16,24,256]{2,1,0:T(8,128)(2,1)}), bf16[16,24,256]{2,1,0:T(8,128)(2,1)S(1)}, u32[]{:S(2)}, u32[]{:S(2)}) %all-to-all-start) | async-done | bytes 196640 | tf_op jit(solution)/shard_map/all_to_all | solution.py:436
  18.8 0.7 copy-done.11
  19.5 2.4 %pack_copies.1 = bf16[8,136,256]{2,1,0:T(8,128)(2,1)} custom-call(s32[5]{0:T(128)} %stack.39.pos, bf16[16,24,256]{2,1,0:T(8,128)(2,1)} %copy-done.11), custom_call_target="tpu_custom_call" | custom-call | tf_op jit(solution)/shard_map/pack_copies/pallas_call | solution.py:202
  21.9 8.2 %all-to-all-start.1 = ((bf16[8,136,256]{2,1,0:T(8,128)(2,1)}), bf16[8,136,256]{2,1,0:T(8,128)(2,1)S(1)}, u32[]{:S(2)}, u32[]{:S(2)}) async-start(bf16[8,136,256]{2,1,0:T(8,128)(2,1)} %pack_copies.1), calls=%async_computation.1 | async-start | bytes 1114112 | tf_op jit(solution)/shard_map/all_to_all | solution.py:438
  30.1 0.7 pad_add_fusion
  30.9 15.6 %all-to-all-done.1.mine_ref = bf16[8,136,256]{2,1,0:T(8,128)(2,1)S(1)} async-done(((bf16[8,136,256]{2,1,0:T(8,128)(2,1)}), bf16[8,136,256]{2,1,0:T(8,128)(2,1)S(1)}, u32[]{:S(2)}, u32[]{:S(2)}) %all-to-all-start.1) | async-done | bytes 557088 | tf_op jit(solution)/shard_map/all_to_all | solution.py:438
  46.5 2.8 %collective-permute-start.4 = (bf16[8,136,256]{2,1,0:T(8,128)(2,1)S(1)}, bf16[8,136,256]{2,1,0:T(8,128)(2,1)S(1)}, u32[]{:S(2)}, u32[]{:S(2)}) collective-permute-start(bf16[8,136,256]{2,1,0:T(8,128)(2,1)S(1)} %all-to-all-done.1.mine_ref), channel_id=1, source_target_pairs={{0,2},{2,0},{1,3},{3,1},{4,6},{6,4},{5,7},{7,5},{8,10},{10,8},{9,1... | collective-permute-start | bytes 1671176 | tf_op jit(solution)/shard_map/ppermute | solution.py:399
  49.3 1.6 convolution_convert_fusion
  51.1 4.7 %collective-permute-done.5 = bf16[64,1024]{1,0:T(8,128)(2,1)S(1)} collective-permute-done((bf16[64,1024]{1,0:T(8,128)(2,1)S(1)}, bf16[64,1024]{1,0:T(8,128)(2,1)S(1)}, u32[]{:S(2)}, u32[]{:S(2)}) %collective-permute-start.5) | collective-permute-done | bytes 131104 | tf_op jit(solution)/shard_map/ppermute | solution.py:399
  55.8 0.9 collective-permute-start.8
  56.8 1.1 collective-permute-start.7
  58.0 1.2 collective-permute-start
  59.2 3.5 %collective-permute-done.8.r3 = bf16[2,64,1024]{2,1,0:T(8,128)(2,1)S(1)} collective-permute-done((bf16[2,64,1024]{2,1,0:T(8,128)(2,1)S(1)}, bf16[2,64,1024]{2,1,0:T(8,128)(2,1)S(1)}, u32[]{:S(2)}, u32[]{:S(2)}) %collective-permute-start.8) | collective-permute-done | bytes 262176 | tf_op jit(solution)/shard_map/ppermute | solution.py:433
  62.7 2.1 %collective-permute-done.7.r2 = bf16[2,64,1024]{2,1,0:T(8,128)(2,1)S(1)} collective-permute-done((bf16[2,64,1024]{2,1,0:T(8,128)(2,1)S(1)}, bf16[2,64,1024]{2,1,0:T(8,128)(2,1)S(1)}, u32[]{:S(2)}, u32[]{:S(2)}) %collective-permute-start.7) | collective-permute-done | bytes 262176 | tf_op jit(solution)/shard_map/ppermute | solution.py:433
  64.9 7.3 %collective-permute-done.6.r1 = bf16[2,64,1024]{2,1,0:T(8,128)(2,1)S(1)} collective-permute-done((bf16[2,64,1024]{2,1,0:T(8,128)(2,1)S(1)}, bf16[2,64,1024]{2,1,0:T(8,128)(2,1)S(1)}, u32[]{:S(2)}, u32[]{:S(2)}) %collective-permute-start.6) | collective-permute-done | bytes 262176 | tf_op jit(solution)/shard_map/ppermute | solution.py:433
  72.1 0.7 copy-done.15
  72.9 0.8 copy-done.5
  73.7 3.7 %heavy_project.1 = (f32[256,256]{1,0:T(8,128)}, bf16[256,256]{1,0:T(8,128)(2,1)}) custom-call(s32[5]{0:T(128)} %stack.39.pos, bf16[8,136,256]{2,1,0:T(8,128)(2,1)} %copy-done.2, bf16[8,136,256]{2,1,0:T(8,128)(2,1)} %copy-done.5, bf16[2,64,1024]{2,1,0:T(8,128)(2,1)} %copy-done.7, bf16[2,64,1024]{2,1,0:T(8,128)(2,1)} %copy-done.15, ...), custom_call_target="tpu_custom_call" | custom-call | tf_op jit(solution)/shard_map/heavy_project/pallas_call | solution.py:251
  77.4 0.9 collective-permute-start.9
  78.3 6.8 %collective-permute-done.9.arrived_ref = bf16[256,256]{1,0:T(8,128)(2,1)S(1)} collective-permute-done((bf16[256,256]{1,0:T(8,128)(2,1)}, bf16[256,256]{1,0:T(8,128)(2,1)S(1)}, u32[]{:S(2)}, u32[]{:S(2)}) %collective-permute-start.9) | collective-permute-done | bytes 131104 | tf_op jit(solution)/shard_map/ppermute | solution.py:399
  85.1 0.7 copy-done.18
  85.8 1.9 %heavy_finish.1 = (bf16[256,128]{1,0:T(8,128)(2,1)}, bf16[8,256,128]{2,1,0:T(8,128)(2,1)}) custom-call(f32[256,256]{1,0:T(8,128)} %get-tuple-element.13.own_ref, bf16[256,256]{1,0:T(8,128)(2,1)} %copy-done.18), custom_call_target="tpu_custom_call" | custom-call | tf_op jit(solution)/shard_map/heavy_finish/pallas_call | solution.py:280
  87.6 3.5 %all-to-all-start.2 = ((bf16[8,256,128]{2,1,0:T(8,128)(2,1)}), bf16[8,256,128]{2,1,0:T(8,128)(2,1)S(1)}, u32[]{:S(2)}, u32[]{:S(2)}) async-start(bf16[8,256,128]{2,1,0:T(8,128)(2,1)} %get-tuple-element.16), calls=%async_computation.2 | async-start | bytes 1048576 | tf_op jit(solution)/shard_map/all_to_all | solution.py:451
  91.1 6.2 %light_project_own.1.part_ref = f32[3,512,512]{2,1,0:T(8,128)} custom-call(s32[5]{0:T(128)} %stack.39.pos, bf16[512,1024]{1,0:T(8,128)(2,1)} %x_ref.1, bf16[3,2048,512]{2,1,0:T(8,128)(2,1)} %w_ref.5), custom_call_target="tpu_custom_call" | custom-call | tf_op jit(solution)/shard_map/light_project_own/pallas_call | solution.py:32
  97.4 1.0 copy-done
  98.4 4.8 %light_project_add.3.kv_ref = bf16[2,512,512]{2,1,0:T(8,128)(2,1)} custom-call(s32[5]{0:T(128)} %stack.39.pos, bf16[512,1024]{1,0:T(8,128)(2,1)} %copy-done, bf16[3,2048,512]{2,1,0:T(8,128)(2,1)} %w_ref.5, f32[3,512,512]{2,1,0:T(8,128)} %light_project_own.1.part_ref), custom_call_target="tpu_custom_call" | custom-call | tf_op jit(solution)/shard_map/light_project_add/pallas_call | solution.py:56
  103.1 1.0 fusion.3
  104.1 4.7 %collective-permute-start.2 = (bf16[2,64,512]{2,1,0:T(8,128)(2,1)S(1)}, bf16[2,64,512]{2,1,0:T(8,128)(2,1)S(1)}, u32[]{:S(2)}, u32[]{:S(2)}) collective-permute-start(bf16[2,64,512]{2,1,0:T(8,128)(2,1)S(1)} %get-tuple-element.17), channel_id=1, source_target_pairs={{2,0},{4,2},{6,4},{8,6},{10,8},{12,10},{14,12},{16,14},{18,16},{20... | collective-permute-start | bytes 393224 | tf_op jit(solution)/shard_map/ppermute | solution.py:463
  108.8 3.4 %collective-permute-start.1 = (bf16[2,64,512]{2,1,0:T(8,128)(2,1)S(1)}, bf16[2,64,512]{2,1,0:T(8,128)(2,1)S(1)}, u32[]{:S(2)}, u32[]{:S(2)}) collective-permute-start(bf16[2,64,512]{2,1,0:T(8,128)(2,1)S(1)} %get-tuple-element.18), channel_id=1, source_target_pairs={{0,2},{2,4},{4,6},{6,8},{8,10},{10,12},{12,14},{14,16},{16,18},{18... | collective-permute-start | bytes 393224 | tf_op jit(solution)/shard_map/ppermute | solution.py:462
  112.3 4.0 %light_project_add.2.q_ref = bf16[1,512,512]{2,1,0:T(8,128)(2,1)} custom-call(s32[5]{0:T(128)} %stack.39.pos, bf16[512,1024]{1,0:T(8,128)(2,1)} %copy-done, bf16[3,2048,512]{2,1,0:T(8,128)(2,1)} %w_ref.5, f32[3,512,512]{2,1,0:T(8,128)} %light_project_own.1.part_ref), custom_call_target="tpu_custom_call" | custom-call | tf_op jit(solution)/shard_map/light_project_add/pallas_call | solution.py:56
  116.3 0.8 slice_reduce_fusion.1
  117.8 0.6 copy-done.17
  118.5 8.5 %light_attention.1 = (f32[512,1024]{1,0:T(8,128)}, bf16[512,1024]{1,0:T(8,128)(2,1)}) custom-call(s32[5]{0:T(128)} %stack.39.pos, bf16[1,512,512]{2,1,0:T(8,128)(2,1)} %light_project_add.2.q_ref, bf16[2,512,512]{2,1,0:T(8,128)(2,1)} %light_project_add.3.kv_ref, bf16[2,64,512]{2,1,0:T(8,128)(2,1)} %copy-done.17, bf16[2,64,512]{2,1,0:T(8,128)(2,1)} %copy-done.16, ...), custom_call_target="tpu_custom_call" | custom-call | tf_op jit(solution)/shard_map/light_attention/pallas_call | solution.py:119
  127.0 1.2 collective-permute-start.3
  128.2 0.8 slice_reduce_fusion
  129.1 0.7 select_n.21.bias_ref
  129.8 2.8 %out_weights.1.w_ref = bf16[2048,128]{1,0:T(8,128)(2,1)} custom-call(s32[5]{0:T(128)} %stack.39.pos, bf16[8,136,256]{2,1,0:T(8,128)(2,1)} %copy-done.2, bf16[8,136,256]{2,1,0:T(8,128)(2,1)} %copy-done.5), custom_call_target="tpu_custom_call" | custom-call | tf_op jit(solution)/shard_map/out_weights/pallas_call | solution.py:308
  132.6 0.8 copy-done.12
  133.4 4.8 %heavy_attention.1 = bf16[16,32,1024]{2,1,0:T(8,128)(2,1)} custom-call(bf16[256,128]{1,0:T(8,128)(2,1)} %get-tuple-element.15.q_ref, bf16[2048,128]{1,0:T(8,128)(2,1)} %bitcast.19, bf16[2048,128]{1,0:T(8,128)(2,1)} %bitcast.21, f32[1,4096]{1,0:T(1,128)} %select_n.21.bias_ref, bf16[2048,128]{1,0:T(8,128)(2,1)} %out_weights.1.w_ref), custom_call_target="tpu_custom_call" | custom-call | tf_op jit(solution)/shard_map/heavy_attention/pallas_call | solution.py:343
  138.3 5.8 %all-to-all-start.3 = ((bf16[16,32,1024]{2,1,0:T(8,128)(2,1)}), bf16[16,32,1024]{2,1,0:T(8,128)(2,1)S(1)}, u32[]{:S(2)}, u32[]{:S(2)}) async-start(bf16[16,32,1024]{2,1,0:T(8,128)(2,1)} %heavy_attention.1), calls=%async_computation.3 | async-start | bytes 2097152 | tf_op jit(solution)/shard_map/all_to_all | solution.py:456
  145.4 7.6 %collective-permute-done.3.recv_ref = bf16[512,1024]{1,0:T(8,128)(2,1)S(1)} collective-permute-done((bf16[512,1024]{1,0:T(8,128)(2,1)}, bf16[512,1024]{1,0:T(8,128)(2,1)S(1)}, u32[]{:S(2)}, u32[]{:S(2)}) %collective-permute-start.3) | collective-permute-done | bytes 1048608 | tf_op jit(solution)/shard_map/ppermute | solution.py:399
  153.0 12.1 %all-to-all-done.3.parts_ref = bf16[16,32,1024]{2,1,0:T(8,128)(2,1)S(1)} async-done(((bf16[16,32,1024]{2,1,0:T(8,128)(2,1)}), bf16[16,32,1024]{2,1,0:T(8,128)(2,1)S(1)}, u32[]{:S(2)}, u32[]{:S(2)}) %all-to-all-start.3) | async-done | bytes 1048608 | tf_op jit(solution)/shard_map/all_to_all | solution.py:456
  165.1 0.8 broadcast_in_dim.15.live_ref
  165.9 0.7 broadcast_in_dim.14.logit_ref
  166.6 4.8 %combine.1 = bf16[512,1024]{1,0:T(8,128)(2,1)} custom-call(f32[512,1024]{1,0:T(8,128)} %get-tuple-element.11.own_ref, bf16[512,1024]{1,0:T(8,128)(2,1)} %copy-done.8, bf16[16,32,1024]{2,1,0:T(8,128)(2,1)} %copy-done.3, f32[32,128]{1,0:T(8,128)} %broadcast_in_dim.14.logit_ref, f32[32,128]{1,0:T(8,128)} %broadcast_in_dim.15.live_ref, s32[1,32]{1,0:T(1,128)} %slots_ref.1), custom_call_target="tpu_custom_call" | custom-call | tf_op jit(solution)/shard_map/combine/pallas_call | solution.py:377
  (52 shorter events, 2.4 us)
Async XLA Ops:
  0.0 58.0 %copy-start.4 = (bf16[512,1024]{1,0:T(8,128)(2,1)S(1)}, bf16[512,1024]{1,0:T(8,128)(2,1)}, u32[]{:S(2)}) copy-start(bf16[512,1024]{1,0:T(8,128)(2,1)} %x_ref.1) | copy-start | bytes 3145732
  4.1 14.8 %all-to-all-start = ((bf16[16,24,256]{2,1,0:T(8,128)(2,1)}), bf16[16,24,256]{2,1,0:T(8,128)(2,1)S(1)}, u32[]{:S(2)}, u32[]{:S(2)}) async-start(bf16[16,24,256]{2,1,0:T(8,128)(2,1)} %pack_heads.1), calls=%async_computation | async-start | bytes 393216 | tf_op jit(solution)/shard_map/all_to_all | solution.py:436
  18.8 0.7 copy-start.11
  21.9 24.5 %all-to-all-start.1 = ((bf16[8,136,256]{2,1,0:T(8,128)(2,1)}), bf16[8,136,256]{2,1,0:T(8,128)(2,1)S(1)}, u32[]{:S(2)}, u32[]{:S(2)}) async-start(bf16[8,136,256]{2,1,0:T(8,128)(2,1)} %pack_copies.1), calls=%async_computation.1 | async-start | bytes 1114112 | tf_op jit(solution)/shard_map/all_to_all | solution.py:438
  46.4 26.4 %copy-start.2 = (bf16[8,136,256]{2,1,0:T(8,128)(2,1)}, bf16[8,136,256]{2,1,0:T(8,128)(2,1)S(1)}, u32[]{:S(2)}) copy-start(bf16[8,136,256]{2,1,0:T(8,128)(2,1)S(1)} %all-to-all-done.1.mine_ref) | copy-start | bytes 1671172
  46.5 26.4 %collective-permute-start.4 = (bf16[8,136,256]{2,1,0:T(8,128)(2,1)S(1)}, bf16[8,136,256]{2,1,0:T(8,128)(2,1)S(1)}, u32[]{:S(2)}, u32[]{:S(2)}) collective-permute-start(bf16[8,136,256]{2,1,0:T(8,128)(2,1)S(1)} %all-to-all-done.1.mine_ref), channel_id=1, source_target_pairs={{0,2},{2,0},{1,3},{3,1},{4,6},{6,4},{5,7},{7,5},{8,10},{10,8},{9,1... | collective-permute-start | bytes 1671176 | tf_op jit(solution)/shard_map/ppermute | solution.py:399
  50.9 7.0 %copy-start.9 = (bf16[64,1024]{1,0:T(8,128)(2,1)}, bf16[64,1024]{1,0:T(8,128)(2,1)S(1)}, u32[]{:S(2)}) copy-start(bf16[64,1024]{1,0:T(8,128)(2,1)S(1)} %convolution_convert_fusion) | copy-start | bytes 393220
  50.9 4.9 %collective-permute-start.5 = (bf16[64,1024]{1,0:T(8,128)(2,1)S(1)}, bf16[64,1024]{1,0:T(8,128)(2,1)S(1)}, u32[]{:S(2)}, u32[]{:S(2)}) collective-permute-start(bf16[64,1024]{1,0:T(8,128)(2,1)S(1)} %convolution_convert_fusion), channel_id=1, source_target_pairs={{0,32},{32,0},{1,33},{33,1},{2,34},{34,2},{3,35},{35,3},{4,36},{36... | collective-permute-start | bytes 393224 | tf_op jit(solution)/shard_map/ppermute | solution.py:399
  55.8 17.0 %copy-start.7 = (bf16[2,64,1024]{2,1,0:T(8,128)(2,1)}, bf16[2,64,1024]{2,1,0:T(8,128)(2,1)S(1)}, u32[]{:S(2)}) copy-start(bf16[2,64,1024]{2,1,0:T(8,128)(2,1)S(1)} %pad_maximum_fusion.r0) | copy-start | bytes 786436
  55.8 6.9 %collective-permute-start.8 = (bf16[2,64,1024]{2,1,0:T(8,128)(2,1)S(1)}, bf16[2,64,1024]{2,1,0:T(8,128)(2,1)S(1)}, u32[]{:S(2)}, u32[]{:S(2)}) collective-permute-start(bf16[2,64,1024]{2,1,0:T(8,128)(2,1)S(1)} %pad_maximum_fusion.r0), channel_id=1, source_target_pairs={{0,192},{64,0},{128,64},{192,128},{1,193},{65,1},{129,65},{193,129... | collective-permute-start | bytes 786440 | tf_op jit(solution)/shard_map/ppermute | solution.py:433
  56.8 8.1 %collective-permute-start.7 = (bf16[2,64,1024]{2,1,0:T(8,128)(2,1)S(1)}, bf16[2,64,1024]{2,1,0:T(8,128)(2,1)S(1)}, u32[]{:S(2)}, u32[]{:S(2)}) collective-permute-start(bf16[2,64,1024]{2,1,0:T(8,128)(2,1)S(1)} %pad_maximum_fusion.r0), channel_id=1, source_target_pairs={{0,128},{64,192},{128,0},{192,64},{1,129},{65,193},{129,1},{193,65... | collective-permute-start | bytes 786440 | tf_op jit(solution)/shard_map/ppermute | solution.py:433
  57.9 14.3 %collective-permute-start.6 = (bf16[2,64,1024]{2,1,0:T(8,128)(2,1)S(1)}, bf16[2,64,1024]{2,1,0:T(8,128)(2,1)S(1)}, u32[]{:S(2)}, u32[]{:S(2)}) collective-permute-start(bf16[2,64,1024]{2,1,0:T(8,128)(2,1)S(1)} %pad_maximum_fusion.r0), channel_id=1, source_target_pairs={{0,64},{64,128},{128,192},{192,0},{1,65},{65,129},{129,193},{193,1... | collective-permute-start | bytes 786440 | tf_op jit(solution)/shard_map/ppermute | solution.py:433
  58.0 39.4 %collective-permute-start = (bf16[512,1024]{1,0:T(8,128)(2,1)S(1)}, bf16[512,1024]{1,0:T(8,128)(2,1)S(1)}, u32[]{:S(2)}, u32[]{:S(2)}) collective-permute-start(bf16[512,1024]{1,0:T(8,128)(2,1)S(1)} %copy-done.4), channel_id=1, source_target_pairs={{0,1},{1,0},{2,3},{3,2},{4,5},{5,4},{6,7},{7,6},{8,9},{9,8},{10,11... | collective-permute-start | bytes 3145736 | tf_op jit(solution)/shard_map/ppermute | solution.py:399
  62.7 9.4 %copy-start.13 = (bf16[2,64,1024]{2,1,0:T(8,128)(2,1)}, bf16[2,64,1024]{2,1,0:T(8,128)(2,1)S(1)}, u32[]{:S(2)}) copy-start(bf16[2,64,1024]{2,1,0:T(8,128)(2,1)S(1)} %collective-permute-done.8.r3) | copy-start | bytes 786436
  64.9 7.3 %copy-start.14 = (bf16[2,64,1024]{2,1,0:T(8,128)(2,1)}, bf16[2,64,1024]{2,1,0:T(8,128)(2,1)S(1)}, u32[]{:S(2)}) copy-start(bf16[2,64,1024]{2,1,0:T(8,128)(2,1)S(1)} %collective-permute-done.7.r2) | copy-start | bytes 786436
  72.1 0.7 copy-start.15
  72.9 0.8 copy-start.5
  77.4 7.7 %collective-permute-start.9 = (bf16[256,256]{1,0:T(8,128)(2,1)}, bf16[256,256]{1,0:T(8,128)(2,1)S(1)}, u32[]{:S(2)}, u32[]{:S(2)}) collective-permute-start(bf16[256,256]{1,0:T(8,128)(2,1)} %get-tuple-element.14), channel_id=1, source_target_pairs={{0,1},{1,0},{2,3},{3,2},{4,5},{5,4},{6,7},{7,6},{8,9},{9,8},{10,11... | collective-permute-start | bytes 393224 | tf_op jit(solution)/shard_map/ppermute | solution.py:399
  85.1 0.7 copy-start.18
  87.6 28.7 %all-to-all-start.2 = ((bf16[8,256,128]{2,1,0:T(8,128)(2,1)}), bf16[8,256,128]{2,1,0:T(8,128)(2,1)S(1)}, u32[]{:S(2)}, u32[]{:S(2)}) async-start(bf16[8,256,128]{2,1,0:T(8,128)(2,1)} %get-tuple-element.16), calls=%async_computation.2 | async-start | bytes 1048576 | tf_op jit(solution)/shard_map/all_to_all | solution.py:451
  97.4 1.0 copy-start
  104.1 13.0 %collective-permute-start.2 = (bf16[2,64,512]{2,1,0:T(8,128)(2,1)S(1)}, bf16[2,64,512]{2,1,0:T(8,128)(2,1)S(1)}, u32[]{:S(2)}, u32[]{:S(2)}) collective-permute-start(bf16[2,64,512]{2,1,0:T(8,128)(2,1)S(1)} %get-tuple-element.17), channel_id=1, source_target_pairs={{2,0},{4,2},{6,4},{8,6},{10,8},{12,10},{14,12},{16,14},{18,16},{20... | collective-permute-start | bytes 393224 | tf_op jit(solution)/shard_map/ppermute | solution.py:463
  108.8 8.4 %collective-permute-start.1 = (bf16[2,64,512]{2,1,0:T(8,128)(2,1)S(1)}, bf16[2,64,512]{2,1,0:T(8,128)(2,1)S(1)}, u32[]{:S(2)}, u32[]{:S(2)}) collective-permute-start(bf16[2,64,512]{2,1,0:T(8,128)(2,1)S(1)} %get-tuple-element.18), channel_id=1, source_target_pairs={{0,2},{2,4},{4,6},{6,8},{8,10},{10,12},{12,14},{14,16},{16,18},{18... | collective-permute-start | bytes 393224 | tf_op jit(solution)/shard_map/ppermute | solution.py:462
  116.3 16.3 %copy-start.6 = (bf16[8,256,128]{2,1,0:T(8,128)(2,1)}, bf16[8,256,128]{2,1,0:T(8,128)(2,1)S(1)}, u32[]{:S(2)}) copy-start(bf16[8,256,128]{2,1,0:T(8,128)(2,1)S(1)} %all-to-all-done.2) | copy-start | bytes 1572868
  116.3 16.3 %collective-permute-start.10 = (bf16[8,256,128]{2,1,0:T(8,128)(2,1)S(1)}, bf16[8,256,128]{2,1,0:T(8,128)(2,1)S(1)}, u32[]{:S(2)}, u32[]{:S(2)}) collective-permute-start(bf16[8,256,128]{2,1,0:T(8,128)(2,1)S(1)} %all-to-all-done.2), channel_id=1, source_target_pairs={{0,2},{2,0},{1,3},{3,1},{4,6},{6,4},{5,7},{7,5},{8,10},{10,8},{9,1... | collective-permute-start | bytes 1572872 | tf_op jit(solution)/shard_map/ppermute | solution.py:399
  117.2 0.7 copy-start.16
  117.8 0.6 copy-start.17
  127.0 26.0 %collective-permute-start.3 = (bf16[512,1024]{1,0:T(8,128)(2,1)}, bf16[512,1024]{1,0:T(8,128)(2,1)S(1)}, u32[]{:S(2)}, u32[]{:S(2)}) collective-permute-start(bf16[512,1024]{1,0:T(8,128)(2,1)} %get-tuple-element.12), channel_id=1, source_target_pairs={{0,1},{1,0},{2,3},{3,2},{4,5},{5,4},{6,7},{7,6},{8,9},{9,8},{10,11... | collective-permute-start | bytes 3145736 | tf_op jit(solution)/shard_map/ppermute | solution.py:399
  129.8 14.9 %copy-start.19 = (bf16[2048]{0:T(1024)(128)(2,1)S(1)}, bf16[2048]{0:T(1024)(128)(2,1)}, u32[]{:S(2)}) copy-start(bf16[2048]{0:T(1024)(128)(2,1)} %param.11) | copy-start | bytes 12292
  129.8 15.0 %copy-start.10 = (bf16[64,1024]{1,0:T(8,128)(2,1)S(1)}, bf16[64,1024]{1,0:T(8,128)(2,1)}, u32[]{:S(2)}) copy-start(bf16[64,1024]{1,0:T(8,128)(2,1)} %copy-done.9) | copy-start | bytes 393220
  129.8 15.2 %copy-start.1 = (bf16[512,1024]{1,0:T(8,128)(2,1)S(1)}, bf16[512,1024]{1,0:T(8,128)(2,1)}, u32[]{:S(2)}) copy-start(bf16[512,1024]{1,0:T(8,128)(2,1)} %copy-done) | copy-start | bytes 3145732
  132.6 0.8 copy-start.12
  138.3 26.8 %all-to-all-start.3 = ((bf16[16,32,1024]{2,1,0:T(8,128)(2,1)}), bf16[16,32,1024]{2,1,0:T(8,128)(2,1)S(1)}, u32[]{:S(2)}, u32[]{:S(2)}) async-start(bf16[16,32,1024]{2,1,0:T(8,128)(2,1)} %heavy_attention.1), calls=%async_computation.3 | async-start | bytes 2097152 | tf_op jit(solution)/shard_map/all_to_all | solution.py:456
  153.0 13.6 %copy-start.8 = (bf16[512,1024]{1,0:T(8,128)(2,1)}, bf16[512,1024]{1,0:T(8,128)(2,1)S(1)}, u32[]{:S(2)}) copy-start(bf16[512,1024]{1,0:T(8,128)(2,1)S(1)} %collective-permute-done.3.recv_ref) | copy-start | bytes 3145732
  165.1 1.5 copy-start.3

commit v2 on v1

v2 whole, which is shorter than its diff:
```python
import functools

import jax
import jax.numpy as jnp
from jax import lax
from jax.experimental import pallas as pl
from jax.experimental.pallas import tpu as pltpu
from jax.sharding import Mesh
from jax.sharding import PartitionSpec as P

HEAD_DIM = 64
RADIUS = 64
NEG = -1e30
SEQ = ("y", "xl", "z", "c")
GROUP = ("y", "xl")


NT = (((1,), (1,)), ((), ()))


def spec(shape, index):
    return pl.BlockSpec(shape, index)


SMALL = pltpu.CompilerParams(vmem_limit_bytes=20 << 20)
HELD = pl.BlockSpec(memory_space=pltpu.VMEM)


def far(a):
    return pltpu.with_memory_space_constraint(a, pltpu.HBM)


def held(a):
    return pltpu.with_memory_space_constraint(a, pltpu.VMEM)


def project_own_kernel(pos, x_ref, w_ref, out_ref):
    out_ref[pl.program_id(0)] = jnp.dot(x_ref[...], w_ref[0], preferred_element_type=jnp.float32)


def project_own(pos, x, w):
    rows, half = x.shape
    cols = w.shape[2]
    return pl.pallas_call(
        project_own_kernel,
        out_shape=pltpu.VMEM((2, rows, cols), jnp.float32),
        grid_spec=pltpu.PrefetchScalarGridSpec(
            num_scalar_prefetch=1,
            grid=(2,),
            in_specs=[
                spec((rows, half), lambda j, p: (0, 0)),
                spec((1, half, cols), lambda j, p: (j + 1, p[1], 0)),
            ],
            out_specs=HELD,
        ),
        compiler_params=SMALL,
        name="light_project_own",
    )(pos, far(x), far(w))


def project_keys_kernel(pos, x_ref, w_ref, part_ref, out_ref, head_ref, tail_ref):
    j = pl.program_id(0)
    rows = out_ref.shape[1]
    total = jnp.dot(x_ref[...], w_ref[0], preferred_element_type=jnp.float32) + part_ref[j]
    total = total.astype(jnp.bfloat16)
    out_ref[j] = total
    head_ref[j] = total[:RADIUS]
    tail_ref[j] = total[rows - RADIUS :]


def project_keys(pos, x, w, part):
    rows, half = x.shape
    cols = w.shape[2]
    return pl.pallas_call(
        project_keys_kernel,
        out_shape=(
            pltpu.VMEM((2, rows, cols), jnp.bfloat16),
            pltpu.VMEM((2, RADIUS, cols), jnp.bfloat16),
            pltpu.VMEM((2, RADIUS, cols), jnp.bfloat16),
        ),
        grid_spec=pltpu.PrefetchScalarGridSpec(
            num_scalar_prefetch=1,
            grid=(2,),
            in_specs=[HELD, spec((1, half, cols), lambda j, p: (j + 1, 1 - p[1], 0)), HELD],
            out_specs=(HELD, HELD, HELD),
        ),
        compiler_params=SMALL,
        name="light_project_keys",
    )(pos, held(x), far(w), held(part))


def project_queries_kernel(pos, own_ref, other_ref, w_ref, out_ref, part_ref):
    step = pl.program_id(0)

    @pl.when(step == 0)
    def _():
        part_ref[...] = jnp.dot(other_ref[...], w_ref[0], preferred_element_type=jnp.float32)

    @pl.when(step == 1)
    def _():
        total = part_ref[...] + jnp.dot(own_ref[...], w_ref[0], preferred_element_type=jnp.float32)
        out_ref[...] = total.astype(jnp.bfloat16)


def project_queries(pos, own, other, w):
    rows, half = own.shape
    cols = w.shape[2]
    return pl.pallas_call(
        project_queries_kernel,
        out_shape=pltpu.VMEM((rows, cols), jnp.bfloat16),
        grid_spec=pltpu.PrefetchScalarGridSpec(
            num_scalar_prefetch=1,
            grid=(2,),
            in_specs=[
                spec((rows, half), lambda k, p: (0, 0)),
                HELD,
                spec((1, half, cols), lambda k, p: (0, jnp.where(k == 0, 1 - p[1], p[1]), 0)),
            ],
            out_specs=HELD,
            scratch_shapes=[pltpu.VMEM((rows, cols), jnp.float32)],
        ),
        compiler_params=SMALL,
        name="light_project_queries",
    )(pos, far(own), held(other), far(w))


def light_block(pos, block, q_ref, kv_ref, left, right, tokens):
    size = 128
    length = kv_ref.shape[1]
    width = q_ref.shape[1]
    span = size + 2 * RADIUS
    low, high = block * size - RADIUS, (block + 1) * size + RADIUS
    row = lax.broadcasted_iota(jnp.int32, (size, span), 0)
    col = lax.broadcasted_iota(jnp.int32, (size, span), 1)
    key = pos[0] * length + low + col
    allowed = (col >= row) & (col - row <= 2 * RADIUS) & (key >= 0) & (key < tokens)
    bias = jnp.where(allowed, 0.0, NEG)
    bias = jnp.concatenate([bias, bias], axis=0)
    lane = lax.broadcasted_iota(jnp.int32, (size, 2 * HEAD_DIM), 1)
    first = lane < HEAD_DIM

    def window(which, lanes):
        pieces = []
        if low < 0:
            pieces.append(left[which, :, lanes])
        pieces.append(kv_ref[which, max(low, 0) : min(high, length), lanes])
        if high > length:
            pieces.append(right[which, :, lanes])
        return pieces[0] if len(pieces) == 1 else jnp.concatenate(pieces, axis=0)

    pieces = []
    for pair in range(width // (2 * HEAD_DIM)):
        lanes = slice(pair * 2 * HEAD_DIM, (pair + 1) * 2 * HEAD_DIM)
        q = q_ref[block * size : (block + 1) * size, lanes]
        k = window(0, lanes)
        v = window(1, lanes)
        zero = jnp.zeros_like(q)
        both = jnp.concatenate([jnp.where(first, q, zero), jnp.where(first, zero, q)], axis=0)
        scores = lax.dot_general(both, k, NT, preferred_element_type=jnp.float32)
        scores = scores * (HEAD_DIM ** -0.5) + bias
        peak = jnp.max(scores, axis=1, keepdims=True)
        weights = jnp.exp(scores - peak)
        total = jnp.sum(weights, axis=1, keepdims=True)
        blended = jnp.dot(weights.astype(jnp.bfloat16), v, preferred_element_type=jnp.float32) / total
        pieces.append(jnp.where(first, blended[:size], blended[size:]).astype(jnp.bfloat16))
    return jnp.concatenate(pieces, axis=1)


def light_kernel(pos, q_ref, kv_ref, left, right, out_ref, *, tokens):
    size = 128
    for block in (1, 2, 0, 3):
        out_ref[block * size : (block + 1) * size, :] = light_block(pos, block, q_ref, kv_ref, left, right, tokens)


def light_attention(pos, q, kv, left, right, tokens):
    return pl.pallas_call(
        functools.partial(light_kernel, tokens=tokens),
        out_shape=pltpu.VMEM(q.shape, jnp.bfloat16),
        grid_spec=pltpu.PrefetchScalarGridSpec(
            num_scalar_prefetch=1,
            grid=(1,),
            in_specs=[HELD] * 4,
            out_specs=HELD,
        ),
        compiler_params=SMALL,
        name="light_attention",
    )(pos, *[held(a) for a in (q, kv, left, right)])


def light_product_kernel(pos, own_ref, recv_ref, own_w_ref, mine_w_ref, theirs_w_ref, out_ref):
    core = pos[2]
    depth = mine_w_ref.shape[0]
    first = recv_ref[:, pl.ds(pl.multiple_of(core * depth, depth), depth)]
    second = recv_ref[:, pl.ds(pl.multiple_of((1 - core) * depth, depth), depth)]
    total = jnp.dot(own_ref[...], own_w_ref[...], preferred_element_type=jnp.float32)
    total = total + jnp.dot(first, mine_w_ref[...], preferred_element_type=jnp.float32)
    out_ref[...] = total + jnp.dot(second, theirs_w_ref[...], preferred_element_type=jnp.float32)


def light_product(pos, own, recv, own_w, mine_w, theirs_w):
    rows, width = own.shape
    half, depth = mine_w.shape[1], mine_w.shape[0]
    block = half // 2
    whole = lambda j, p: (0, 0)
    column = lambda j, p: (0, j)
    return pl.pallas_call(
        light_product_kernel,
        out_shape=jax.ShapeDtypeStruct((rows, half), jnp.float32),
        grid_spec=pltpu.PrefetchScalarGridSpec(
            num_scalar_prefetch=1,
            grid=(2,),
            in_specs=[
                spec((rows, width), whole),
                spec((rows, width), whole),
                spec((width, block), lambda j, p: (0, 2 * p[1] + j)),
                spec((depth, block), column),
                spec((depth, block), column),
            ],
            out_specs=spec((rows, block), column),
        ),
        compiler_params=SMALL,
        name="light_product",
    )(pos, own, recv, far(own_w), mine_w, theirs_w)


def pack_heads_kernel(counts, qkv_ref, out_w_ref, packed_ref):
    depth = qkv_ref.shape[1]
    heads = qkv_ref.shape[2] // HEAD_DIM
    turned = out_w_ref[...]
    shape = (packed_ref.shape[1] - depth, packed_ref.shape[2])
    marks = jnp.where(lax.broadcasted_iota(jnp.int32, shape, 1) < 2 * HEAD_DIM, counts[0], counts[1])
    marks = marks.astype(jnp.float32).astype(jnp.bfloat16)
    for h in range(heads):
        lanes = slice(h * HEAD_DIM, (h + 1) * HEAD_DIM)
        piece = jnp.concatenate([qkv_ref[0, :, lanes], turned[:, lanes], qkv_ref[1, :, lanes], qkv_ref[2, :, lanes]], axis=1)
        for side in range(2):
            packed_ref[2 * h + side, 0:depth, :] = piece
            packed_ref[2 * h + side, depth:, :] = marks


def pack_heads(count, qkv, out_w):
    depth = qkv.shape[1]
    heads = qkv.shape[2] // HEAD_DIM
    return pl.pallas_call(
        pack_heads_kernel,
        out_shape=jax.ShapeDtypeStruct((2 * heads, depth + 8, 4 * HEAD_DIM), jnp.bfloat16),
        grid_spec=pltpu.PrefetchScalarGridSpec(
            num_scalar_prefetch=1,
            grid=(1,),
            in_specs=[spec(qkv.shape, lambda i, p: (0, 0, 0)), spec(out_w.shape, lambda i, p: (0, 0))],
            out_specs=spec((2 * heads, depth + 8, 4 * HEAD_DIM), lambda i, p: (0, 0, 0)),
        ),
        compiler_params=SMALL,
        name="pack_heads",
    )(count, far(qkv), far(out_w))


def pack_copies_kernel(pos, in_ref, out_ref, *, depth):
    side = pos[1]
    copies = out_ref.shape[0]
    group = in_ref.shape[0] // 2
    lane = lax.broadcasted_iota(jnp.int32, (depth, 4 * HEAD_DIM), 1)
    from_out = (lane >= HEAD_DIM) & (lane < 2 * HEAD_DIM)
    marks = []
    for i in range(group):
        qkv = in_ref[side * group + i, 0:depth, :]
        out_w = in_ref[2 * i + side, 0:depth, :]
        tile = jnp.where(from_out, out_w, qkv)
        marks.append(in_ref[2 * i + side, depth : depth + 1, :])
        for t in range(copies):
            out_ref[t, i * depth : (i + 1) * depth, :] = tile
    marks = jnp.concatenate(marks, axis=0)
    for t in range(copies):
        out_ref[t, group * depth :, :] = marks


def pack_copies(pos, sliced, copies):
    group = sliced.shape[0] // 2
    depth = sliced.shape[1] - 8
    shape = (copies, group * depth + group, 4 * HEAD_DIM)
    return pl.pallas_call(
        functools.partial(pack_copies_kernel, depth=depth),
        out_shape=jax.ShapeDtypeStruct(shape, jnp.bfloat16),
        grid_spec=pltpu.PrefetchScalarGridSpec(
            num_scalar_prefetch=1,
            grid=(1,),
            in_specs=[HELD],
            out_specs=spec(shape, lambda i, p: (0, 0, 0)),
        ),
        compiler_params=SMALL,
        name="pack_copies",
    )(pos, held(sliced))


def heavy_project_kernel(
    pos, mine_ref, theirs_ref, r0, r1, r2, r3, router_ref, own_ref, other_ref, w_ref, *, depth, capacity
):
    side, core, y, xl = pos[1], pos[2], pos[3], pos[4]
    z_size = mine_ref.shape[0]
    for y_half in range(2):
        for x in range(2):
            for m in range(2):
                i = (y_half * 2 + x) * 2 + m
                for z in range(z_size):
                    base = ((y_half * 2 + x) * z_size + z) * 2
                    w_ref[m, pl.ds(pl.multiple_of((base + core) * depth, depth), depth), :] = mine_ref[
                        z, i * depth : (i + 1) * depth, :
                    ]
                    w_ref[m, pl.ds(pl.multiple_of((base + 1 - core) * depth, depth), depth), :] = theirs_ref[
                        z, i * depth : (i + 1) * depth, :
                    ]
    lane = lax.broadcasted_iota(jnp.int32, (capacity, 2 * HEAD_DIM), 1)
    keep = lane < HEAD_DIM
    upper = lane < HEAD_DIM + HEAD_DIM // 2
    own_w = w_ref[side]
    other_w = w_ref[1 - side]
    for d, piece in enumerate((r0, r1, r2, r3)):
        rows = piece[...].reshape(4 * capacity, piece.shape[2])
        for_other = jnp.dot(rows, other_w, preferred_element_type=jnp.float32)
        for_own = jnp.dot(rows, own_w, preferred_element_type=jnp.float32)
        score = jnp.dot(rows, router_ref[...], preferred_element_type=jnp.float32)
        high = score.astype(jnp.bfloat16).astype(jnp.float32)
        source_y = lax.rem(y - d + 4, 4)
        for which in range(2):
            source = source_y * 2 + (xl if which == 0 else 1 - xl)
            query = slice(which * 2 * capacity, which * 2 * capacity + capacity)
            keys = slice(query.stop, query.stop + capacity)
            at = pl.ds(pl.multiple_of(source * capacity, capacity), capacity)
            terms = jnp.where(upper, high[query], score[query] - high[query])
            left = jnp.where(keep, for_other[query, : 2 * HEAD_DIM], terms)
            other_ref[at, :] = jnp.concatenate([left, for_other[keys, 2 * HEAD_DIM :]], axis=1).astype(jnp.bfloat16)
            left = jnp.where(keep, for_own[query, : 2 * HEAD_DIM], score[query])
            own_ref[at, :] = jnp.concatenate([left, for_own[keys, 2 * HEAD_DIM :]], axis=1)


def heavy_project(pos, mine, theirs, pieces, router, depth):
    capacity = pieces[0].shape[1] // 2
    half = pieces[0].shape[2]
    slots = 8 * capacity
    return pl.pallas_call(
        functools.partial(heavy_project_kernel, depth=depth, capacity=capacity),
        out_shape=(
            pltpu.VMEM((slots, 4 * HEAD_DIM), jnp.float32),
            pltpu.VMEM((slots, 4 * HEAD_DIM), jnp.bfloat16),
        ),
        grid_spec=pltpu.PrefetchScalarGridSpec(
            num_scalar_prefetch=1,
            grid=(1,),
            in_specs=[HELD] * (3 + len(pieces)),
            out_specs=(HELD, HELD),
            scratch_shapes=[pltpu.VMEM((2, half, 4 * HEAD_DIM), jnp.bfloat16)],
        ),
        compiler_params=SMALL,
        name="heavy_project",
    )(pos, held(mine), held(theirs), *[held(p) for p in pieces], held(router))


def finish_kernel(pos, own_ref, arrived_ref, mine_ref, query_ref, gate_ref, copies_ref, *, capacity):
    own = own_ref[...]
    arrived = arrived_ref[...].astype(jnp.float32)
    total = (own + arrived).astype(jnp.bfloat16)
    lane = lax.broadcasted_iota(jnp.int32, (own.shape[0], 2 * HEAD_DIM), 1)
    query_ref[...] = jnp.where(lane < HEAD_DIM, total[:, : 2 * HEAD_DIM].astype(jnp.float32), 0.0).astype(jnp.bfloat16)
    for t in range(copies_ref.shape[0]):
        copies_ref[t] = total[:, 2 * HEAD_DIM :]
    middle = HEAD_DIM + HEAD_DIM // 2
    logit = own[:, HEAD_DIM : HEAD_DIM + 1] + arrived[:, HEAD_DIM : HEAD_DIM + 1] + arrived[:, middle : middle + 1]
    gate = jnp.broadcast_to(1.0 / (1.0 + jnp.exp(-logit)), gate_ref.shape)
    group = own.shape[0] // capacity
    tail = mine_ref.shape[1] - group
    marks = mine_ref[pos[5], tail:, 2 * HEAD_DIM :].astype(jnp.float32)
    slot = lax.broadcasted_iota(jnp.int32, (capacity, 2 * HEAD_DIM), 0).astype(jnp.float32)
    for g in range(group):
        rows = slice(g * capacity, (g + 1) * capacity)
        gate_ref[rows, :] = jnp.where(slot < marks[g : g + 1, :], gate[rows], 0.0)


def finish(pos, own, arrived, mine, capacity):
    slots = own.shape[0]
    copies = mine.shape[0]
    return pl.pallas_call(
        functools.partial(finish_kernel, capacity=capacity),
        out_shape=(
            pltpu.VMEM((slots, 2 * HEAD_DIM), jnp.bfloat16),
            pltpu.VMEM((slots, 2 * HEAD_DIM), jnp.float32),
            pltpu.HBM((copies, slots, 2 * HEAD_DIM), jnp.bfloat16),
        ),
        grid_spec=pltpu.PrefetchScalarGridSpec(
            num_scalar_prefetch=1,
            grid=(1,),
            in_specs=[HELD, HELD, HELD],
            out_specs=(HELD, HELD, spec((copies, slots, 2 * HEAD_DIM), lambda i, p: (0, 0, 0))),
        ),
        compiler_params=SMALL,
        name="heavy_finish",
    )(pos, held(own), held(arrived), held(mine))


def out_weights_kernel(pos, mine_ref, theirs_ref, out_ref, bias_ref, *, depth, capacity):
    core = pos[2]
    z_size = mine_ref.shape[0]
    group = 8
    for i in range(group):
        for z in range(z_size):
            base = (i * z_size + z) * 2
            tile = slice(i * depth, (i + 1) * depth)
            out_ref[pl.ds(pl.multiple_of((base + core) * depth, depth), depth), :] = mine_ref[z, tile, : 2 * HEAD_DIM]
            out_ref[pl.ds(pl.multiple_of((base + 1 - core) * depth, depth), depth), :] = theirs_ref[
                z, tile, : 2 * HEAD_DIM
            ]
    lane = lax.broadcasted_iota(jnp.int32, (1, 2 * HEAD_DIM), 1)
    per_row = 2 * HEAD_DIM // capacity
    for which, ref in enumerate((mine_ref, theirs_ref)):
        for z in range(z_size):
            marks = ref[z, group * depth : group * depth + group, : 2 * HEAD_DIM].astype(jnp.float32)
            for part in range(group // per_row):
                count = jnp.zeros((1, 2 * HEAD_DIM), jnp.float32)
                for j in range(per_row):
                    g = part * per_row + j
                    count = jnp.where(lane // capacity == j, marks[g : g + 1, :], count)
                live = (lane % capacity).astype(jnp.float32) < count
                at = ((which * z_size + z) * (group // per_row) + part) * 2 * HEAD_DIM
                bias_ref[:, at : at + 2 * HEAD_DIM] = jnp.where(live, 0.0, NEG)


def out_weights(pos, mine, theirs, depth, capacity):
    z_size = mine.shape[0]
    return pl.pallas_call(
        functools.partial(out_weights_kernel, depth=depth, capacity=capacity),
        out_shape=(
            pltpu.VMEM((16 * z_size * depth, 2 * HEAD_DIM), jnp.bfloat16),
            pltpu.VMEM((1, 16 * z_size * capacity), jnp.float32),
        ),
        grid_spec=pltpu.PrefetchScalarGridSpec(
            num_scalar_prefetch=1,
            grid=(1,),
            in_specs=[HELD, HELD],
            out_specs=(HELD, HELD),
        ),
        compiler_params=SMALL,
        name="out_weights",
    )(pos, held(mine), held(theirs))


def heavy_kernel(q_ref, own_ref, other_ref, bias_ref, w_ref, gate_ref, out_ref):
    keys = own_ref.shape[0]
    q = q_ref[...]
    lane = lax.broadcasted_iota(jnp.int32, (1, 2 * HEAD_DIM), 1)
    scale = HEAD_DIM ** -0.5
    s0 = lax.dot_general(q, own_ref[...], NT, preferred_element_type=jnp.float32) * scale + bias_ref[:, :keys]
    s1 = lax.dot_general(q, other_ref[...], NT, preferred_element_type=jnp.float32) * scale + bias_ref[:, keys:]
    peak = jnp.maximum(jnp.max(s0, axis=1, keepdims=True), jnp.max(s1, axis=1, keepdims=True))
    p0 = jnp.exp(s0 - peak)
    p1 = jnp.exp(s1 - peak)
    total = jnp.sum(p0, axis=1, keepdims=True) + jnp.sum(p1, axis=1, keepdims=True)
    blended = jnp.dot(p0.astype(jnp.bfloat16), own_ref[...], preferred_element_type=jnp.float32)
    blended = blended + jnp.dot(p1.astype(jnp.bfloat16), other_ref[...], preferred_element_type=jnp.float32)
    context = jnp.where(lane >= HEAD_DIM, blended / total, 0.0).astype(jnp.bfloat16)
    part = lax.dot_general(context, w_ref[...], NT, preferred_element_type=jnp.float32)
    part = (part * gate_ref[:, 0:1]).astype(jnp.bfloat16)
    count, capacity, half = out_ref.shape
    for i in range(count):
        top = i // 2 * capacity
        out_ref[i] = part[top : top + capacity, i % 2 * half : (i % 2 + 1) * half]


def heavy_attention(q, own, other, bias, w, gate, group):
    return pl.pallas_call(
        heavy_kernel,
        out_shape=jax.ShapeDtypeStruct((2 * group, q.shape[0] // group, w.shape[0] // 2), jnp.bfloat16),
        in_specs=[HELD] * 6,
        compiler_params=SMALL,
        name="heavy_attention",
    )(*[held(a) for a in (q, own, other, bias, w, gate)])


def combine_kernel(own_ref, parts_ref, slots_ref, out_ref, hi_ref, lo_ref):
    step = pl.program_id(0)
    block = out_ref.shape[0]

    @pl.when(step == 0)
    def _():
        total = parts_ref[0].astype(jnp.float32)
        for i in range(1, parts_ref.shape[0]):
            total = total + parts_ref[i].astype(jnp.float32)
        hi = total.astype(jnp.bfloat16)
        hi_ref[...] = hi
        lo_ref[...] = (total - hi.astype(jnp.float32)).astype(jnp.bfloat16)

    capacity = slots_ref.shape[1]
    token = lax.broadcasted_iota(jnp.int32, (block, capacity), 0) + step * block
    pick = jnp.where(token == slots_ref[...], 1.0, 0.0).astype(jnp.bfloat16)
    heavy = jnp.dot(pick, hi_ref[...], preferred_element_type=jnp.float32)
    heavy = heavy + jnp.dot(pick, lo_ref[...], preferred_element_type=jnp.float32)
    out_ref[...] = (own_ref[...] + heavy).astype(jnp.bfloat16)


def combine(own, parts, slots):
    rows, cols = own.shape
    capacity = slots.shape[1]
    block = 128
    return pl.pallas_call(
        combine_kernel,
        out_shape=jax.ShapeDtypeStruct((rows, cols), jnp.bfloat16),
        grid=(rows // block,),
        in_specs=[spec((block, cols), lambda b: (b, 0)), HELD, spec((1, capacity), lambda b: (0, 0))],
        out_specs=spec((block, cols), lambda b: (b, 0)),
        scratch_shapes=[
            pltpu.VMEM((capacity, cols), jnp.bfloat16),
            pltpu.VMEM((capacity, cols), jnp.bfloat16),
        ],
        compiler_params=SMALL,
        name="combine",
    )(own, held(parts), slots)


def swap(a, axis):
    return lax.ppermute(a, axis, [(0, 1), (1, 0)])


def layer(
    normed,
    router,
    light_qkv,
    light_out,
    heavy_qkv,
    heavy_out,
    query_slots,
    query_count,
    key_slots,
    key_count,
):
    rows, half = normed.shape
    side = lax.axis_index("xh")
    core = lax.axis_index("c")
    shard_index = lax.axis_index(SEQ)
    shard_total = lax.axis_size(SEQ)
    y_size, _, z_size, _ = (lax.axis_size(axis) for axis in SEQ)
    capacity = query_slots.shape[1]
    feature_rows = heavy_qkv.shape[1]
    heads = heavy_qkv.shape[2] // HEAD_DIM
    group = heads
    pos = jnp.stack([shard_index, side, core, lax.axis_index("y"), lax.axis_index("xl"), lax.axis_index("z")]).astype(jnp.int32)

    slots = jnp.concatenate([query_slots[0], key_slots[0]])
    pick = (slots[:, None] == jnp.arange(rows, dtype=jnp.int32)[None, :]).astype(jnp.bfloat16)
    routed = jnp.dot(pick, normed, preferred_element_type=jnp.float32).astype(jnp.bfloat16)
    partner = swap(routed, "xl")
    pair = jnp.stack([routed, partner])
    router_own = lax.dynamic_slice_in_dim(router, side * half, half, 0)
    router_own = jnp.broadcast_to(router_own[:, None], (half, 2 * HEAD_DIM))
    pieces = [pair]
    for d in range(1, y_size):
        pieces.append(lax.ppermute(pair, "y", [(i, (i + d) % y_size) for i in range(y_size)]))

    by_head = pack_heads(jnp.concatenate([key_count, query_count]), heavy_qkv, jnp.transpose(heavy_out))
    sliced = lax.all_to_all(by_head, GROUP + ("xh",), 0, 0)
    packed = pack_copies(pos, sliced, z_size)
    mine = lax.all_to_all(packed, "z", 0, 0)
    theirs = swap(mine, "c")
    out_all, bias = out_weights(pos, mine, theirs, feature_rows, capacity)

    part_own, part_other = heavy_project(pos, mine, theirs, pieces, router_own, feature_rows)
    arrived = swap(part_other, "xh")
    query, gate, copies = finish(pos, part_own, arrived, mine, capacity)
    keys_own = lax.all_to_all(copies, "z", 0, 0)
    keys_other = swap(keys_own, "c")
    keys_own = keys_own.reshape(-1, 2 * HEAD_DIM)
    keys_other = keys_other.reshape(-1, 2 * HEAD_DIM)
    outputs = heavy_attention(query, keys_own, keys_other, bias, out_all, gate, group)
    parts = lax.all_to_all(outputs, GROUP + ("xh",), 0, 0)

    features = swap(normed, "xh")
    partial = project_own(pos, normed, light_qkv)
    paired, head, tail = project_keys(pos, features, light_qkv, partial)
    ends = shard_total - 1
    left = lax.ppermute(tail, SEQ, [(i, i + 1) for i in range(ends)])
    right = lax.ppermute(head, SEQ, [(i + 1, i) for i in range(ends)])
    queries = project_queries(pos, normed, features, light_qkv)
    context = light_attention(pos, queries, paired, left, right, rows * shard_total)
    context_recv = swap(context, "xh")

    depth = light_out.shape[0] // 2
    cut = lax.dynamic_slice(light_out, (core * depth, (1 - side) * half), (depth, half))
    mine_w = lax.ppermute(cut, ("xl", "xh"), [(i, 3 - i) for i in range(4)])
    theirs_w = swap(mine_w, "c")
    own = light_product(pos, context, context_recv, light_out, mine_w, theirs_w)
    return combine(own, parts, query_slots)


def solution(mesh):
    fine = Mesh(mesh.devices.reshape(4, 2, 8, 2, 2), SEQ + ("xh",))
    in_specs = (
        P(SEQ, "xh"),
        P(),
        P(None, None, "xh"),
        P("xh", None),
        P(None, SEQ, "xh"),
        P("xh", SEQ),
        P(SEQ, None),
        P(SEQ),
        P(SEQ, None),
        P(SEQ),
    )
    return jax.shard_map(layer, mesh=fine, in_specs=in_specs, out_specs=P(SEQ, "xh"), check_vma=False)
```

time: 172 us -> 155 us (0.901)
  the two profiles are of different devices: /device:TPU:1 before, /device:TPU:8 now
where the time goes in v2:
time: 155 us
  waiting for transfers between devices  75.2 us (49%)
  starting transfers between devices  46 us (30%)
  Pallas kernels  28.1 us (18%)
  local copies, waits for them, and re-layouts  3.15 us (2%)
  between operations  1.58 us (1%)
    ppermute x7, waiting for transfers between devices, swap(): return lax.ppermute(a, axis, [(0, 1), (1, 0)])  24.2 us
    all_to_all x1, waiting for transfers between devices, layer(): mine = lax.all_to_all(packed, 'z', 0, 0)  16.7 us
    all_to_all x1, waiting for transfers between devices, layer(): keys_own = lax.all_to_all(copies, 'z', 0, 0)  16 us
    ppermute x3, waiting for transfers between devices, layer(): lax.ppermute(pair, 'y', [(i, (i + d) % y_size) for i in range(y_size)])  11.5 us
    all_to_all x1, starting transfers between devices, layer(): mine = lax.all_to_all(packed, 'z', 0, 0)  8.47 us
    all_to_all x1, starting transfers between devices, layer(): sliced = lax.all_to_all(by_head, GROUP + ('xh',), 0, 0)  7.39 us
    all_to_all x1, waiting for transfers between devices, layer(): sliced = lax.all_to_all(by_head, GROUP + ('xh',), 0, 0)  6.79 us
    all_to_all x1, starting transfers between devices, layer(): parts = lax.all_to_all(outputs, GROUP + ('xh',), 0, 0)  6.67 us
  transfers between devices with their start and end apart: 17, of which 9 were waited for; matrix products, arithmetic and copies ran while one was open for 2% of the time, Pallas kernels for 12%

profile of v2, /device:TPU:8, one launch (start us, length us, event | category | flops | bytes accessed | tf_op | source)
XLA Modules:
  0.0 154.5 jit_solution(1465209499276070497)
XLA Ops:
  1.4 0.1 pad_add_fusion.counts
  1.5 2.1 %pack_heads.1 = bf16[16,24,256]{2,1,0:T(8,128)(2,1)} custom-call(s32[2]{0:T(128)S(1)} %pad_add_fusion.counts, bf16[3,16,512]{2,1,0:T(8,128)(2,1)} %qkv_ref.1, bf16[16,512]{1,0:T(8,128)(2,1)} %bitcast.19), custom_call_target="tpu_custom_call" | custom-call | tf_op jit(solution)/shard_map/pack_heads/pallas_call | solution.py:244
  3.6 7.4 %all-to-all-start = ((bf16[16,24,256]{2,1,0:T(8,128)(2,1)}), bf16[16,24,256]{2,1,0:T(8,128)(2,1)S(1)}, u32[]{:S(2)}, u32[]{:S(2)}) async-start(bf16[16,24,256]{2,1,0:T(8,128)(2,1)} %pack_heads.1), calls=%async_computation | async-start | bytes 393216 | tf_op jit(solution)/shard_map/all_to_all | solution.py:557
  11.0 0.1 stack.36.pos
  11.0 6.8 %all-to-all-done.in_ref = bf16[16,24,256]{2,1,0:T(8,128)(2,1)S(1)} async-done(((bf16[16,24,256]{2,1,0:T(8,128)(2,1)}), bf16[16,24,256]{2,1,0:T(8,128)(2,1)S(1)}, u32[]{:S(2)}, u32[]{:S(2)}) %all-to-all-start) | async-done | bytes 196640 | tf_op jit(solution)/shard_map/all_to_all | solution.py:557
  17.8 1.4 pack_copies.1
  19.2 8.5 %all-to-all-start.1 = ((bf16[8,136,256]{2,1,0:T(8,128)(2,1)}), bf16[8,136,256]{2,1,0:T(8,128)(2,1)S(1)}, u32[]{:S(2)}, u32[]{:S(2)}) async-start(bf16[8,136,256]{2,1,0:T(8,128)(2,1)} %pack_copies.1), calls=%async_computation.1 | async-start | bytes 1114112 | tf_op jit(solution)/shard_map/all_to_all | solution.py:559
  27.7 0.1 pad_add_fusion.1
  27.8 16.7 %all-to-all-done.1.mine_ref = bf16[8,136,256]{2,1,0:T(8,128)(2,1)S(1)} async-done(((bf16[8,136,256]{2,1,0:T(8,128)(2,1)}), bf16[8,136,256]{2,1,0:T(8,128)(2,1)S(1)}, u32[]{:S(2)}, u32[]{:S(2)}) %all-to-all-start.1) | async-done | bytes 557088 | tf_op jit(solution)/shard_map/all_to_all | solution.py:559
  44.5 0.0 collective-permute-start.6
  44.5 0.3 convolution_convert_fusion
  44.8 0.7 collective-permute-start.7
  45.5 5.3 %collective-permute-done.7 = bf16[64,1024]{1,0:T(8,128)(2,1)S(1)} collective-permute-done((bf16[64,1024]{1,0:T(8,128)(2,1)S(1)}, bf16[64,1024]{1,0:T(8,128)(2,1)S(1)}, u32[]{:S(2)}, u32[]{:S(2)}) %collective-permute-start.7) | collective-permute-done | bytes 131104 | tf_op jit(solution)/shard_map/ppermute | solution.py:518
  50.8 1.1 collective-permute-start.8
  51.9 2.7 %collective-permute-start.9 = (bf16[2,64,1024]{2,1,0:T(8,128)(2,1)S(1)}, bf16[2,64,1024]{2,1,0:T(8,128)(2,1)S(1)}, u32[]{:S(2)}, u32[]{:S(2)}) collective-permute-start(bf16[2,64,1024]{2,1,0:T(8,128)(2,1)S(1)} %pad_maximum_fusion.r0), channel_id=1, source_target_pairs={{0,128},{64,192},{128,0},{192,64},{1,129},{65,193},{129,1},{193,65... | collective-permute-start | bytes 786440 | tf_op jit(solution)/shard_map/ppermute | solution.py:554
  54.6 0.5 collective-permute-start.10
  55.1 5.0 %collective-permute-done.8.r1 = bf16[2,64,1024]{2,1,0:T(8,128)(2,1)S(1)} collective-permute-done((bf16[2,64,1024]{2,1,0:T(8,128)(2,1)S(1)}, bf16[2,64,1024]{2,1,0:T(8,128)(2,1)S(1)}, u32[]{:S(2)}, u32[]{:S(2)}) %collective-permute-start.8) | collective-permute-done | bytes 262176 | tf_op jit(solution)/shard_map/ppermute | solution.py:554
  60.1 2.5 %collective-permute-done.9.r2 = bf16[2,64,1024]{2,1,0:T(8,128)(2,1)S(1)} collective-permute-done((bf16[2,64,1024]{2,1,0:T(8,128)(2,1)S(1)}, bf16[2,64,1024]{2,1,0:T(8,128)(2,1)S(1)}, u32[]{:S(2)}, u32[]{:S(2)}) %collective-permute-start.9) | collective-permute-done | bytes 262176 | tf_op jit(solution)/shard_map/ppermute | solution.py:554
  62.6 4.0 %collective-permute-done.10.r3 = bf16[2,64,1024]{2,1,0:T(8,128)(2,1)S(1)} collective-permute-done((bf16[2,64,1024]{2,1,0:T(8,128)(2,1)S(1)}, bf16[2,64,1024]{2,1,0:T(8,128)(2,1)S(1)}, u32[]{:S(2)}, u32[]{:S(2)}) %collective-permute-start.10) | collective-permute-done | bytes 262176 | tf_op jit(solution)/shard_map/ppermute | solution.py:554
  66.6 0.0 collective-permute-done.6.theirs_ref
  66.6 0.2 broadcast_in_dim.2.router_ref
  66.8 1.6 %heavy_project.1 = (f32[256,256]{1,0:T(8,128)S(1)}, bf16[256,256]{1,0:T(8,128)(2,1)S(1)}) custom-call(s32[6]{0:T(128)S(1)} %stack.36.pos, bf16[8,136,256]{2,1,0:T(8,128)(2,1)S(1)} %all-to-all-done.1.mine_ref, bf16[8,136,256]{2,1,0:T(8,128)(2,1)S(1)} %collective-permute-done.6.theirs_ref, bf16[2,64,1024]{2,1,0:T(8,128)(2,1)S(1)} %pad_maximum_fusion.r0, ...), custom_call_target="tpu_custom_call" | custom-call | tf_op jit(solution)/shard_map/heavy_project/pallas_call | solution.py:340
  68.4 1.0 collective-permute-start.11
  69.4 6.0 %collective-permute-done.11.arrived_ref = bf16[256,256]{1,0:T(8,128)(2,1)S(1)} collective-permute-done((bf16[256,256]{1,0:T(8,128)(2,1)S(1)}, bf16[256,256]{1,0:T(8,128)(2,1)S(1)}, u32[]{:S(2)}, u32[]{:S(2)}) %collective-permute-start.11) | collective-permute-done | bytes 131104 | tf_op jit(solution)/shard_map/ppermute | solution.py:518
  75.5 1.4 heavy_finish.1
  76.8 3.5 %all-to-all-start.2 = ((bf16[8,256,128]{2,1,0:T(8,128)(2,1)}), bf16[8,256,128]{2,1,0:T(8,128)(2,1)S(1)}, u32[]{:S(2)}, u32[]{:S(2)}) async-start(bf16[8,256,128]{2,1,0:T(8,128)(2,1)} %get-tuple-element.21), calls=%async_computation.2 | async-start | bytes 1048576 | tf_op jit(solution)/shard_map/all_to_all | solution.py:566
  80.3 1.0 collective-permute-start
  81.3 16.0 %all-to-all-done.2 = bf16[8,256,128]{2,1,0:T(8,128)(2,1)S(1)} async-done(((bf16[8,256,128]{2,1,0:T(8,128)(2,1)}), bf16[8,256,128]{2,1,0:T(8,128)(2,1)S(1)}, u32[]{:S(2)}, u32[]{:S(2)}) %all-to-all-start.2) | async-done | bytes 524320 | tf_op jit(solution)/shard_map/all_to_all | solution.py:566
  97.4 1.9 %dynamic_slice.6 = bf16[256,1024]{1,0:T(8,128)(2,1)} dynamic-slice(bf16[512,2048]{1,0:T(8,128)(2,1)} %own_w_ref.1, s32[]{:T(128)S(6)} %select_n.9, s32[]{:T(128)S(6)} %select_n.10), dynamic_slice_sizes={256,1024} | dynamic-slice | bytes 1048580 | tf_op jit(solution)/shard_map/dynamic_slice | solution.py:584
  99.2 1.1 collective-permute-start.4
  100.4 0.7 out_weights.1
  101.1 2.5 %heavy_attention.1 = bf16[16,32,1024]{2,1,0:T(8,128)(2,1)S(1)} custom-call(bf16[256,128]{1,0:T(8,128)(2,1)S(1)} %get-tuple-element.20.q_ref, bf16[2048,128]{1,0:T(8,128)(2,1)S(1)} %bitcast.14, bf16[2048,128]{1,0:T(8,128)(2,1)S(1)} %bitcast.15, f32[1,4096]{1,0:T(1,128)S(1)} %get-tuple-element.22.bias_ref, bf16[2048,128]{1,0:T(8,128)(2,1)S(1)} %get-tuple-element.23.w_ref, ...), custom_call_target="tpu_custom_call" | custom-call | tf_op jit(solution)/shard_map/heavy_attention/pallas_call | solution.py:468
  103.6 0.0 copy-start
  103.6 1.0 copy-done
  104.5 6.7 %all-to-all-start.3 = ((bf16[16,32,1024]{2,1,0:T(8,128)(2,1)}), bf16[16,32,1024]{2,1,0:T(8,128)(2,1)S(1)}, u32[]{:S(2)}, u32[]{:S(2)}) async-start(bf16[16,32,1024]{2,1,0:T(8,128)(2,1)} %copy-done), calls=%async_computation.3 | async-start | bytes 2097152 | tf_op jit(solution)/shard_map/all_to_all | solution.py:571
  111.2 3.5 %light_project_own.1.part_ref = f32[2,512,512]{2,1,0:T(8,128)S(1)} custom-call(s32[6]{0:T(128)S(1)} %stack.36.pos, bf16[512,1024]{1,0:T(8,128)(2,1)} %x_ref.1, bf16[3,2048,512]{2,1,0:T(8,128)(2,1)} %w_ref.5), custom_call_target="tpu_custom_call" | custom-call | tf_op jit(solution)/shard_map/light_project_own/pallas_call | solution.py:44
  114.8 0.0 collective-permute-done.other_ref.x_ref
  114.8 3.2 %light_project_keys.1 = (bf16[2,512,512]{2,1,0:T(8,128)(2,1)S(1)}, bf16[2,64,512]{2,1,0:T(8,128)(2,1)S(1)}, bf16[2,64,512]{2,1,0:T(8,128)(2,1)S(1)}) custom-call(s32[6]{0:T(128)S(1)} %stack.36.pos, bf16[512,1024]{1,0:T(8,128)(2,1)S(1)} %collective-permute-done.other_ref.x_ref, bf16[3,2048,512]{2,1,0:T(8,128)(2,1)} %w_ref.5, ...), custom_call_target="tpu_custom_call" | custom-call | tf_op jit(solution)/shard_map/light_project_keys/pallas_call | solution.py:74
  118.0 1.9 %collective-permute-start.1 = (bf16[2,64,512]{2,1,0:T(8,128)(2,1)S(1)}, bf16[2,64,512]{2,1,0:T(8,128)(2,1)S(1)}, u32[]{:S(2)}, u32[]{:S(2)}) collective-permute-start(bf16[2,64,512]{2,1,0:T(8,128)(2,1)S(1)} %get-tuple-element.16), channel_id=1, source_target_pairs={{0,2},{2,4},{4,6},{6,8},{8,10},{10,12},{12,14},{14,16},{16,18},{18... | collective-permute-start | bytes 393224 | tf_op jit(solution)/shard_map/ppermute | solution.py:577
  119.9 6.7 %collective-permute-start.2 = (bf16[2,64,512]{2,1,0:T(8,128)(2,1)S(1)}, bf16[2,64,512]{2,1,0:T(8,128)(2,1)S(1)}, u32[]{:S(2)}, u32[]{:S(2)}) collective-permute-start(bf16[2,64,512]{2,1,0:T(8,128)(2,1)S(1)} %get-tuple-element.17), channel_id=1, source_target_pairs={{2,0},{4,2},{6,4},{8,6},{10,8},{12,10},{14,12},{16,14},{18,16},{20... | collective-permute-start | bytes 393224 | tf_op jit(solution)/shard_map/ppermute | solution.py:578
  126.6 0.3 collective-permute-start.5
  126.9 3.6 %light_project_queries.1.q_ref = bf16[512,512]{1,0:T(8,128)(2,1)S(1)} custom-call(s32[6]{0:T(128)S(1)} %stack.36.pos, bf16[512,1024]{1,0:T(8,128)(2,1)} %x_ref.1, bf16[512,1024]{1,0:T(8,128)(2,1)S(1)} %collective-permute-done.other_ref.x_ref, bf16[3,2048,512]{2,1,0:T(8,128)(2,1)} %w_ref.5), custom_call_target="tpu_custom_call" | custom-call | tf_op jit(solution)/shard_map/light_project_queries/pallas_call | solution.py:108
  130.5 0.0 collective-permute-done.1.left
  130.5 2.5 %light_attention.1.own_ref = bf16[512,512]{1,0:T(8,128)(2,1)S(1)} custom-call(s32[6]{0:T(128)S(1)} %stack.36.pos, bf16[512,512]{1,0:T(8,128)(2,1)S(1)} %light_project_queries.1.q_ref, bf16[2,512,512]{2,1,0:T(8,128)(2,1)S(1)} %get-tuple-element.15.kv_ref, bf16[2,64,512]{2,1,0:T(8,128)(2,1)S(1)} %collective-permute-done.1.left, ...), custom_call_target="tpu_custom_call" | custom-call | tf_op jit(solution)/shard_map/light_attention/pallas_call | solution.py:176
  132.9 3.1 %collective-permute-start.3 = (bf16[512,512]{1,0:T(8,128)(2,1)S(1)}, bf16[512,512]{1,0:T(8,128)(2,1)S(1)}, u32[]{:S(2)}, u32[]{:S(2)}) collective-permute-start(bf16[512,512]{1,0:T(8,128)(2,1)S(1)} %light_attention.1.own_ref), channel_id=1, source_target_pairs={{0,1},{1,0},{2,3},{3,2},{4,5},{5,4},{6,7},{7,6},{8,9},{9,8},{10,11... | collective-permute-start | bytes 1572872 | tf_op jit(solution)/shard_map/ppermute | solution.py:518
  136.0 12.9 %collective-permute-done.3.recv_ref = bf16[512,512]{1,0:T(8,128)(2,1)S(1)} collective-permute-done((bf16[512,512]{1,0:T(8,128)(2,1)S(1)}, bf16[512,512]{1,0:T(8,128)(2,1)S(1)}, u32[]{:S(2)}, u32[]{:S(2)}) %collective-permute-start.3) | collective-permute-done | bytes 524320 | tf_op jit(solution)/shard_map/ppermute | solution.py:518
  148.8 3.2 %light_product.1.own_ref = f32[512,1024]{1,0:T(8,128)S(1)} custom-call(s32[6]{0:T(128)S(1)} %stack.36.pos, bf16[512,512]{1,0:T(8,128)(2,1)S(1)} %light_attention.1.own_ref, bf16[512,512]{1,0:T(8,128)(2,1)S(1)} %collective-permute-done.3.recv_ref, bf16[512,2048]{1,0:T(8,128)(2,1)} %own_w_ref.1, bf16[256,1024]{1,0:T(8,128)(2,1)} %collective-permute-done.4.mine_w_ref, ...), custom_call_target="tpu_custom_call" | custom-call | tf_op jit(solution)/shard_map/light_product/pallas_call | solution.py:206
  152.1 2.4 %combine.1 = bf16[512,1024]{1,0:T(8,128)(2,1)} custom-call(f32[512,1024]{1,0:T(8,128)S(1)} %light_product.1.own_ref, bf16[16,32,1024]{2,1,0:T(8,128)(2,1)S(1)} %all-to-all-done.3.parts_ref, s32[1,32]{1,0:T(1,128)S(1)} %copy-done.1), custom_call_target="tpu_custom_call" | custom-call | tf_op jit(solution)/shard_map/combine/pallas_call | solution.py:502
  (16 shorter events, 0.1 us)
Async XLA Ops:
  0.0 27.7 %copy-start.4 = (s32[1,32]{1,0:T(1,128)S(1)}, s32[1,32]{1,0:T(1,128)}, u32[]{:S(2)}) copy-start(s32[1,32]{1,0:T(1,128)} %param.18) | copy-start | bytes 388
  0.0 27.7 %copy-start.1 = (s32[1,32]{1,0:T(1,128)S(1)}, s32[1,32]{1,0:T(1,128)}, u32[]{:S(2)}) copy-start(s32[1,32]{1,0:T(1,128)} %slots_ref.1) | copy-start | bytes 388
  0.0 44.5 %copy-start.2 = (bf16[512,1024]{1,0:T(8,128)(2,1)S(1)}, bf16[512,1024]{1,0:T(8,128)(2,1)}, u32[]{:S(2)}) copy-start(bf16[512,1024]{1,0:T(8,128)(2,1)} %x_ref.1) | copy-start | bytes 3145732
  1.5 53.6 %copy-start.3 = (bf16[2048]{0:T(1024)(128)(2,1)S(1)}, bf16[2048]{0:T(1024)(128)(2,1)}, u32[]{:S(2)}) copy-start(bf16[2048]{0:T(1024)(128)(2,1)} %param.11) | copy-start | bytes 12292
  3.6 14.3 %all-to-all-start = ((bf16[16,24,256]{2,1,0:T(8,128)(2,1)}), bf16[16,24,256]{2,1,0:T(8,128)(2,1)S(1)}, u32[]{:S(2)}, u32[]{:S(2)}) async-start(bf16[16,24,256]{2,1,0:T(8,128)(2,1)} %pack_heads.1), calls=%async_computation | async-start | bytes 393216 | tf_op jit(solution)/shard_map/all_to_all | solution.py:557
  19.2 25.2 %all-to-all-start.1 = ((bf16[8,136,256]{2,1,0:T(8,128)(2,1)}), bf16[8,136,256]{2,1,0:T(8,128)(2,1)S(1)}, u32[]{:S(2)}, u32[]{:S(2)}) async-start(bf16[8,136,256]{2,1,0:T(8,128)(2,1)} %pack_copies.1), calls=%async_computation.1 | async-start | bytes 1114112 | tf_op jit(solution)/shard_map/all_to_all | solution.py:559
  44.5 22.1 %collective-permute-start.6 = (bf16[8,136,256]{2,1,0:T(8,128)(2,1)S(1)}, bf16[8,136,256]{2,1,0:T(8,128)(2,1)S(1)}, u32[]{:S(2)}, u32[]{:S(2)}) collective-permute-start(bf16[8,136,256]{2,1,0:T(8,128)(2,1)S(1)} %all-to-all-done.1.mine_ref), channel_id=1, source_target_pairs={{0,2},{2,0},{1,3},{3,1},{4,6},{6,4},{5,7},{7,5},{8,10},{10,8},{9,1... | collective-permute-start | bytes 1671176 | tf_op jit(solution)/shard_map/ppermute | solution.py:518
  44.8 6.0 %collective-permute-start.7 = (bf16[64,1024]{1,0:T(8,128)(2,1)S(1)}, bf16[64,1024]{1,0:T(8,128)(2,1)S(1)}, u32[]{:S(2)}, u32[]{:S(2)}) collective-permute-start(bf16[64,1024]{1,0:T(8,128)(2,1)S(1)} %convolution_convert_fusion), channel_id=1, source_target_pairs={{0,32},{32,0},{1,33},{33,1},{2,34},{34,2},{3,35},{35,3},{4,36},{36... | collective-permute-start | bytes 393224 | tf_op jit(solution)/shard_map/ppermute | solution.py:518
  50.8 9.3 %collective-permute-start.8 = (bf16[2,64,1024]{2,1,0:T(8,128)(2,1)S(1)}, bf16[2,64,1024]{2,1,0:T(8,128)(2,1)S(1)}, u32[]{:S(2)}, u32[]{:S(2)}) collective-permute-start(bf16[2,64,1024]{2,1,0:T(8,128)(2,1)S(1)} %pad_maximum_fusion.r0), channel_id=1, source_target_pairs={{0,64},{64,128},{128,192},{192,0},{1,65},{65,129},{129,193},{193,1... | collective-permute-start | bytes 786440 | tf_op jit(solution)/shard_map/ppermute | solution.py:554
  51.9 10.7 %collective-permute-start.9 = (bf16[2,64,1024]{2,1,0:T(8,128)(2,1)S(1)}, bf16[2,64,1024]{2,1,0:T(8,128)(2,1)S(1)}, u32[]{:S(2)}, u32[]{:S(2)}) collective-permute-start(bf16[2,64,1024]{2,1,0:T(8,128)(2,1)S(1)} %pad_maximum_fusion.r0), channel_id=1, source_target_pairs={{0,128},{64,192},{128,0},{192,64},{1,129},{65,193},{129,1},{193,65... | collective-permute-start | bytes 786440 | tf_op jit(solution)/shard_map/ppermute | solution.py:554
  54.6 12.0 %collective-permute-start.10 = (bf16[2,64,1024]{2,1,0:T(8,128)(2,1)S(1)}, bf16[2,64,1024]{2,1,0:T(8,128)(2,1)S(1)}, u32[]{:S(2)}, u32[]{:S(2)}) collective-permute-start(bf16[2,64,1024]{2,1,0:T(8,128)(2,1)S(1)} %pad_maximum_fusion.r0), channel_id=1, source_target_pairs={{0,192},{64,0},{128,64},{192,128},{1,193},{65,1},{129,65},{193,129... | collective-permute-start | bytes 786440 | tf_op jit(solution)/shard_map/ppermute | solution.py:554
  68.4 7.0 %collective-permute-start.11 = (bf16[256,256]{1,0:T(8,128)(2,1)S(1)}, bf16[256,256]{1,0:T(8,128)(2,1)S(1)}, u32[]{:S(2)}, u32[]{:S(2)}) collective-permute-start(bf16[256,256]{1,0:T(8,128)(2,1)S(1)} %get-tuple-element.19), channel_id=1, source_target_pairs={{0,1},{1,0},{2,3},{3,2},{4,5},{5,4},{6,7},{7,6},{8,9},{9,8},{10,11... | collective-permute-start | bytes 393224 | tf_op jit(solution)/shard_map/ppermute | solution.py:518
  76.8 20.5 %all-to-all-start.2 = ((bf16[8,256,128]{2,1,0:T(8,128)(2,1)}), bf16[8,256,128]{2,1,0:T(8,128)(2,1)S(1)}, u32[]{:S(2)}, u32[]{:S(2)}) async-start(bf16[8,256,128]{2,1,0:T(8,128)(2,1)} %get-tuple-element.21), calls=%async_computation.2 | async-start | bytes 1048576 | tf_op jit(solution)/shard_map/all_to_all | solution.py:566
  80.3 34.4 %collective-permute-start = (bf16[512,1024]{1,0:T(8,128)(2,1)}, bf16[512,1024]{1,0:T(8,128)(2,1)S(1)}, u32[]{:S(2)}, u32[]{:S(2)}) collective-permute-start(bf16[512,1024]{1,0:T(8,128)(2,1)} %x_ref.1), channel_id=1, source_target_pairs={{0,1},{1,0},{2,3},{3,2},{4,5},{5,4},{6,7},{7,6},{8,9},{9,8},{10,11... | collective-permute-start | bytes 3145736 | tf_op jit(solution)/shard_map/ppermute | solution.py:518
  97.4 3.7 %collective-permute-start.12 = (bf16[8,256,128]{2,1,0:T(8,128)(2,1)S(1)}, bf16[8,256,128]{2,1,0:T(8,128)(2,1)S(1)}, u32[]{:S(2)}, u32[]{:S(2)}) collective-permute-start(bf16[8,256,128]{2,1,0:T(8,128)(2,1)S(1)} %all-to-all-done.2), channel_id=1, source_target_pairs={{0,2},{2,0},{1,3},{3,1},{4,6},{6,4},{5,7},{7,5},{8,10},{10,8},{9,1... | collective-permute-start | bytes 1572872 | tf_op jit(solution)/shard_map/ppermute | solution.py:518
  99.2 27.4 %collective-permute-start.4 = (bf16[256,1024]{1,0:T(8,128)(2,1)}, bf16[256,1024]{1,0:T(8,128)(2,1)}, u32[]{:S(2)}, u32[]{:S(2)}) collective-permute-start(bf16[256,1024]{1,0:T(8,128)(2,1)} %dynamic_slice.6), channel_id=1, source_target_pairs={{0,33},{1,32},{32,1},{33,0},{2,35},{3,34},{34,3},{35,2},{4,37},{5,... | collective-permute-start | bytes 1572872 | tf_op jit(solution)/shard_map/ppermute | solution.py:585
  103.6 1.0 copy-start
  104.5 47.6 %all-to-all-start.3 = ((bf16[16,32,1024]{2,1,0:T(8,128)(2,1)}), bf16[16,32,1024]{2,1,0:T(8,128)(2,1)S(1)}, u32[]{:S(2)}, u32[]{:S(2)}) async-start(bf16[16,32,1024]{2,1,0:T(8,128)(2,1)} %copy-done), calls=%async_computation.3 | async-start | bytes 2097152 | tf_op jit(solution)/shard_map/all_to_all | solution.py:571
  118.0 12.4 %collective-permute-start.1 = (bf16[2,64,512]{2,1,0:T(8,128)(2,1)S(1)}, bf16[2,64,512]{2,1,0:T(8,128)(2,1)S(1)}, u32[]{:S(2)}, u32[]{:S(2)}) collective-permute-start(bf16[2,64,512]{2,1,0:T(8,128)(2,1)S(1)} %get-tuple-element.16), channel_id=1, source_target_pairs={{0,2},{2,4},{4,6},{6,8},{8,10},{10,12},{12,14},{14,16},{16,18},{18... | collective-permute-start | bytes 393224 | tf_op jit(solution)/shard_map/ppermute | solution.py:577
  119.9 10.5 %collective-permute-start.2 = (bf16[2,64,512]{2,1,0:T(8,128)(2,1)S(1)}, bf16[2,64,512]{2,1,0:T(8,128)(2,1)S(1)}, u32[]{:S(2)}, u32[]{:S(2)}) collective-permute-start(bf16[2,64,512]{2,1,0:T(8,128)(2,1)S(1)} %get-tuple-element.17), channel_id=1, source_target_pairs={{2,0},{4,2},{6,4},{8,6},{10,8},{12,10},{14,12},{16,14},{18,16},{20... | collective-permute-start | bytes 393224 | tf_op jit(solution)/shard_map/ppermute | solution.py:578
  126.6 9.4 %collective-permute-start.5 = (bf16[256,1024]{1,0:T(8,128)(2,1)}, bf16[256,1024]{1,0:T(8,128)(2,1)S(1)}, u32[]{:S(2)}, u32[]{:S(2)}) collective-permute-start(bf16[256,1024]{1,0:T(8,128)(2,1)} %collective-permute-done.4.mine_w_ref), channel_id=1, source_target_pairs={{0,2},{2,0},{1,3},{3,1},{4,6},{6,4},{5,7},{7,5},{8,10},{10,8},{9,1... | collective-permute-start | bytes 1572872 | tf_op jit(solution)/shard_map/ppermute | solution.py:518
  132.9 15.9 %collective-permute-start.3 = (bf16[512,512]{1,0:T(8,128)(2,1)S(1)}, bf16[512,512]{1,0:T(8,128)(2,1)S(1)}, u32[]{:S(2)}, u32[]{:S(2)}) collective-permute-start(bf16[512,512]{1,0:T(8,128)(2,1)S(1)} %light_attention.1.own_ref), channel_id=1, source_target_pairs={{0,1},{1,0},{2,3},{3,2},{4,5},{5,4},{6,7},{7,6},{8,9},{9,8},{10,11... | collective-permute-start | bytes 1572872 | tf_op jit(solution)/shard_map/ppermute | solution.py:518
